TPU v7x, 256 devices: a whole 4x4x8 slice. The times are simulated.
256 devices in a mesh: dp: 4 (over x), expert: 64 (over z, y, core).
Axes of the slice: x: 4, y: 4, z: 8, core: 2. Of those that a mesh axis runs over, the one named last changes fastest.
Arguments:
- saved_inputs: bfloat16 [3, 65536, 1024], P(None, ('dp', 'expert')), may hold values from -6 to 6
- cotangent: bfloat16 [65536, 1024], P(('dp', 'expert')), may hold values from -6 to 6
- weight_in: bfloat16 [128, 1024, 1024], P('expert'), may hold values from -0.1875 to 0.1875
- weight_out: bfloat16 [128, 512, 1024], P('expert'), may hold values from -0.25 to 0.25
- expert_ids: int32 [3, 65536, 1], P(None, ('dp', 'expert')), may hold values from 0 to 127; in each aligned block of 256 rows (0 to 255, 256 to 511, ..., all dimensions but the last counted through in order) at most 4 rows name the same one
Outputs:
- input_grad: bfloat16 [65536, 1024], P(('dp', 'expert'))
- weight_in_grad: float32 [128, 1024, 1024], P('expert', 'dp')
- weight_out_grad: float32 [128, 512, 1024], P('expert', 'dp')
Inputs may be any that keep to these rules, and one draw needn't show every extreme that they name: `expert_ids`: in each step, at most 4 of the 256 tokens of one device name the same expert, and some device reaches 4.
All inputs are finite; a program needn't handle non-finite values.
Results may differ from a plain program's by a relative error of at most 0.014.
Values may be sent and summed in bfloat16 or wider, within the bound.
No kernel may reach another device: no remote copies, remote signals or barrier semaphores. Data moves between devices by JAX's collectives and lax.ppermute only.
A program may use at most 128 MiB of HBM per device.

v0:
```python
import functools

import jax
import jax.numpy as jnp
from jax import lax
from jax.experimental import pallas as pl
from jax.experimental.pallas import tpu as pltpu
from jax.sharding import PartitionSpec as P


D = 1024
H = 512
STEPS = 3
MOST = 4
NY, NC = 4, 2
BF = jnp.bfloat16
F32 = jnp.float32
NN = (((1,), (0,)), ((), ()))
NT = (((1,), (1,)), ((), ()))
TN = (((0,), (0,)), ((), ()))
shape = jax.ShapeDtypeStruct


def call(kernel, outs, *args, spaces=None, out_spaces=None, scratch=()):
    place = {"v": pltpu.VMEM, "s": pltpu.SMEM, "h": pltpu.HBM}
    spaces, out_spaces = spaces or "v" * len(args), out_spaces or "v" * len(outs)
    ins = [pl.BlockSpec(memory_space=place[c]) for c in spaces]
    args = [pltpu.with_memory_space_constraint(a, pltpu.HBM) if c == "h" else a for a, c in zip(args, spaces)]
    outs = tuple(pltpu.HBM(o.shape, o.dtype) if c == "h" else o for o, c in zip(outs, out_spaces))
    return pl.pallas_call(
        kernel,
        out_shape=outs,
        in_specs=ins,
        out_specs=tuple(pl.BlockSpec(memory_space=place[c]) for c in out_spaces),
        scratch_shapes=list(scratch),
        compiler_params=pltpu.CompilerParams(vmem_limit_bytes=24 << 20),
    )(*args)


class Copies:
    def __init__(self, sems, first=0):
        self.sems, self.count, self.open = sems, first, []

    def start(self, src, dst):
        one = pltpu.make_async_copy(src, dst, self.sems.at[self.count])
        self.count += 1
        one.start()
        return one

    def store(self, src, dst):
        self.open.append(self.start(src, dst))

    def finish(self):
        for one in self.open:
            one.wait()


def copies_of(e, pairs, sems, first):
    each = len(pairs)
    return [pltpu.make_async_copy(a.at[e], b.at[e], sems.at[first + each * e + i]) for i, (a, b) in enumerate(pairs)]


def dot(a, b, dims=NN):
    return lax.dot_general(a, b, dims, preferred_element_type=F32)


def loop(count, step):
    lax.fori_loop(0, count, lambda i, c: (step(i), c)[1], 0)


def block(i, size):
    return pl.ds(pl.multiple_of(i * size, size), size)


def slot_of(ids, experts):
    tokens = ids.shape[1]
    onehot = (ids[:, :, None] == jnp.arange(experts, dtype=jnp.int32)).astype(BF)
    earlier = (jnp.arange(tokens)[:, None] > jnp.arange(tokens)[None, :]).astype(BF)
    before = jnp.einsum("ts,kse->kte", earlier, onehot, preferred_element_type=F32)
    rank = jnp.sum(before * onehot.astype(F32), axis=2).astype(jnp.int32)
    return ids * MOST + rank


def picked(row, rows, start, count):
    sel = lax.broadcasted_iota(jnp.int32, (count, row.shape[1]), 0) + start == row
    return dot(sel.astype(BF), rows).astype(BF)


def pack_kernel(steps, row_ref, x_ref, *outs):
    for n, out in enumerate(outs):
        size = out.shape[0] // len(steps)
        per = size // 256

        def part(i):
            k = i // per
            step = steps[0] - k
            x = x_ref[step] if len(x_ref.shape) == 3 else x_ref[...]
            out[block(i, 256)] = picked(row_ref[pl.ds(step, 1)], x, n * size + i % per * 256, 256)

        loop(per * len(steps), part)


def mix_kernel(start, own_ref, other_ref, *outs):
    n = outs[0].shape[0] // 2
    for i, out in enumerate(outs):
        out[:n] = own_ref[start + i * n : start + (i + 1) * n]
        out[n:] = other_ref[start + i * n : start + (i + 1) * n]


def turn_kernel(parts, *refs):
    ins, outs = refs[:parts], refs[parts:]
    ny = len(outs)

    def pieces(ref):
        return ref[...].astype(F32).reshape(NC, ny, 8, D)

    rows = [pieces(r) for r in ins]
    for y, out in enumerate(outs):
        out[...] = jnp.concatenate([r[c, y] for r in rows for c in range(NC)], axis=0).astype(BF)


def home_kernel(step, send, row_ref, col_ref, back_ref, g_hbm, *refs):
    if send:
        g_out, pack_out, old_ref, new_ref, pack_ref, sems = refs
    else:
        g_out, old_ref, new_ref, sems = refs
    copies = Copies(sems)
    load = copies.start(g_hbm, old_ref)
    slots, tokens = back_ref.shape[0], old_ref.shape[0]
    sel = (col_ref[:, step : step + 1] == lax.broadcasted_iota(jnp.int32, (tokens, slots), 1)).astype(BF)
    load.wait()

    def add(i):
        cols = block(i, 128)
        fresh = old_ref[:, cols].astype(F32) + dot(sel, back_ref[:, cols])
        new_ref[:, cols] = fresh.astype(BF)

    loop(D // 128, add)
    copies.store(new_ref, g_out)
    if send:
        count = slots // 128

        def chunk(i):
            return pltpu.make_async_copy(
                pack_ref.at[block(i, 128)], pack_out.at[block(i, 128)], sems.at[copies.count + i]
            )

        def part(i):
            pack_ref[block(i, 128)] = picked(row_ref[step - 1 : step], new_ref[...], i * 128, 128)
            chunk(i).start()

        loop(count, part)
        loop(count, lambda i: chunk(i).wait())
    copies.finish()


def tick_kernel(ref, out):
    out[...] = ref[...]


def swap_halves(low, a, b):
    return jnp.where(low, a, pltpu.roll(b, 4, 0)), jnp.where(low, pltpu.roll(a, 4, 0), b)


def by_expert(load, count, rows_ref):
    low = lax.broadcasted_iota(jnp.int32, (8, D), 0) < 4

    def four(q):
        a, b, c, d = load(q)
        a0, a1 = swap_halves(low, a, b)
        c0, c1 = swap_halves(low, c, d)
        rows_ref[0, block(q, 16)] = jnp.concatenate([a0, c0], axis=0).astype(BF)
        rows_ref[1, block(q, 16)] = jnp.concatenate([a1, c1], axis=0).astype(BF)

    loop(count // 4, four)


def tiles(ref):
    def load(q):
        rows = ref[block(q, 32)].astype(F32)
        return [rows[i * 8 : (i + 1) * 8] for i in range(4)]

    return load


def x_math(w_hbm, w_ref, scratch, outs, sems):
    x_ref = scratch[0]
    experts = x_ref.shape[0]
    results = list(zip(scratch, outs))

    def expert(e):
        for one in copies_of(e, [(w_hbm, w_ref)], sems, 0):
            one.wait()

        def part(i):
            take, c = block(i % 4, x_ref.shape[1] // 4), i // 4
            cols, ups = block(c, 256), pl.ds(pl.multiple_of(H + c * 256, 256), 256)
            rows = x_ref[e, take]
            gate = dot(rows, w_ref[e, :, cols])
            up = dot(rows, w_ref[e, :, ups])
            s = jax.nn.sigmoid(gate)
            silu = gate * s
            scratch[1][e, take, cols] = silu.astype(BF)
            scratch[2][e, take, cols] = (up * s * (1.0 + gate * (1.0 - s))).astype(BF)
            scratch[3][e, take, cols] = (silu * up).astype(BF)

        loop(4 * (H // 256), part)
        for one in copies_of(e, results, sems, experts):
            one.start()

    loop(experts, expert)
    for e in range(experts):
        for one in copies_of(e, results, sems, experts):
            one.wait()


def load_weights(w_hbm, w_ref, sems):
    for e in range(w_ref.shape[0]):
        for one in copies_of(e, [(w_hbm, w_ref)], sems, 0):
            one.start()


def x_kernel(parts, where_ref, *refs):
    chunks, w_hbm, refs = refs[:parts], refs[parts], refs[parts + 1 :]
    outs, scratch, (w_ref, sems, blocks_ref) = refs[:4], refs[4:8], refs[8:]
    load_weights(w_hbm, w_ref, sems)
    at = 0
    for chunk in chunks:
        n = chunk.shape[0] // 8

        def part(i):
            blocks_ref[pl.ds(at + i * 4, 4)] = chunk[block(i, 32)].astype(F32).reshape(4, 8, D)

        loop(n // 4, part)
        at += n

    def load(q):
        return [blocks_ref[where_ref[4 * q + i]] for i in range(4)]

    by_expert(load, blocks_ref.shape[0], scratch[0])
    x_math(w_hbm, w_ref, scratch, outs, sems)


def g_kernel(keep, g_in, silu_hbm, slope_hbm, win_hbm, wout_hbm, *refs):
    if keep:
        g_ref, pre_ref, back_out = refs[:3]
    else:
        g_out, pre_out, back_out, g_ref, pre_ref = refs[:5]
    silu_ref, slope_ref, win_ref, wout_ref, exp_ref, back_ref, sems = refs[-7:]
    experts = g_ref.shape[0]
    first = [(wout_hbm, wout_ref), (silu_hbm, silu_ref), (slope_hbm, slope_ref)]
    second = [(win_hbm, win_ref)]
    results = [] if keep else [(g_ref, g_out), (pre_ref, pre_out)]
    base = experts * len(first)
    after = base + experts
    for e in range(experts):
        for one in copies_of(e, first, sems, 0) + copies_of(e, second, sems, base):
            one.start()
    by_expert(tiles(g_in), g_in.shape[0] // 8, g_ref)

    def expert(e):
        for one in copies_of(e, first, sems, 0):
            one.wait()

        def inner(i):
            take, c = block(i % 2, g_ref.shape[1] // 2), i // 2
            cols, ups = block(c, 256), pl.ds(pl.multiple_of(H + c * 256, 256), 256)
            grad = dot(g_ref[e, take], wout_ref[e, cols], NT)
            pre_ref[e, take, cols] = (grad * slope_ref[e, take, cols].astype(F32)).astype(BF)
            pre_ref[e, take, ups] = (grad * silu_ref[e, take, cols].astype(F32)).astype(BF)

        loop(2 * (H // 256), inner)
        for one in copies_of(e, results, sems, after):
            one.start()
        for one in copies_of(e, second, sems, base):
            one.wait()

        def outer(i):
            cols = block(i, 256)
            exp_ref[e, :, cols] = dot(pre_ref[e], win_ref[e, cols], NT)

        loop(D // 256, outer)

    loop(experts, expert)
    low = lax.broadcasted_iota(jnp.int32, (8, D), 0) < 4
    count = exp_ref.shape[1] // 8
    last = after + experts * len(results)
    pieces = 4

    def back(q):
        e0, e1 = exp_ref[0, block(q, 8)], exp_ref[1, block(q, 8)]
        a, b = swap_halves(low, e0, e1)
        back_ref[block(q, 16)] = jnp.concatenate([a, b], axis=0).astype(BF)

    def piece(i):
        rows = block(i, 16 * count // pieces)
        return pltpu.make_async_copy(back_ref.at[rows], back_out.at[rows], sems.at[last + i])

    def send(i):
        loop(count // pieces, lambda q: back(i * (count // pieces) + q))
        piece(i).start()

    loop(pieces, send)
    loop(pieces, lambda i: piece(i).wait())
    for e in range(experts):
        for one in copies_of(e, results, sems, after):
            one.wait()


def grad_kernel(picks, dp, turn_ref, *refs):
    steps = [refs[4 * k : 4 * k + 4] for k in range(STEPS)]
    adds, outs = refs[4 * STEPS : -2], refs[-2:]
    rows_in, rows_out = D // dp, H // dp
    (e0, r0), (e1, r1) = picks

    def one_slice(n):
        e, place = e0 + n * (e1 - e0), turn_ref[r0 + n * (r1 - r0)]
        lefts = [(x[e, :, block(place, rows_in)], hid[e, :, block(place, rows_out)]) for x, _, hid, _ in steps]

        def part(i):
            cols = block(i, 256)
            one = sum(dot(left[0], pre[e, :, cols], TN) for left, (_, pre, _, _) in zip(lefts, steps))
            two = sum(dot(left[1], g[e, :, cols], TN) for left, (_, _, _, g) in zip(lefts, steps))
            for m, out in enumerate(outs):

                @pl.when(n == m)
                def _():
                    first, second = one, two
                    if adds:
                        first = first + adds[m][:rows_in, cols].astype(F32)
                        second = second + adds[m][rows_in:, cols].astype(F32)
                    out[:rows_in, cols] = first.astype(out.dtype)
                    out[rows_in:, cols] = second.astype(out.dtype)

        loop(D // 256, part)

    loop(2, one_slice)


def final_kernel(count, *refs):
    ins, (win_out, wout_out) = refs[:-2], refs[-2:]
    rows_in = win_out.shape[1]
    for e in range(win_out.shape[0]):
        group = ins[e * count : (e + 1) * count]

        def part(i):
            rows = block(i, 32)
            win_out[e, rows] = sum(ref[rows].astype(F32) for ref in group)

        loop(rows_in // 32, part)

        def rest(i):
            rows = block(i, 32)
            later = pl.ds(pl.multiple_of(rows_in + i * 32, 32), 32)
            wout_out[e, rows] = sum(ref[later].astype(F32) for ref in group)

        loop(wout_out.shape[1] // 32, rest)


def program(saved_inputs, cotangent, weight_in, weight_out, expert_ids):
    peers = lax.axis_size("expert")
    dp = lax.axis_size("dp")
    exp_dev = weight_in.shape[0]
    experts = exp_dev * peers
    tokens = saved_inputs.shape[1]
    slots = experts * MOST
    per_dev = exp_dev * MOST
    plane = NY * NC
    nz = peers // plane

    me = lax.axis_index("expert").astype(jnp.int32)
    here = lax.axis_index("dp").astype(jnp.int32)
    turns = (here + jnp.arange(dp, dtype=jnp.int32)) % dp

    def apart(target, source):
        dz = (target // plane - source // plane) % nz
        dy = (target // NC % NY - source // NC % NY) % NY
        dc = (target % NC - source % NC) % NC
        return dz, dy, dc

    place = slot_of(expert_ids[:, :, 0], experts)
    column = place.T
    dz, dy, dc = apart(place // per_dev, me)
    place_near = ((dc * nz + dz) * NY + dy) * per_dev + place % per_dev
    sources = jnp.arange(peers, dtype=jnp.int32)
    dz, dy, dc = apart(me, sources)
    block_of = (dy * nz + dz) * NC + dc

    def swap(rows):
        per = rows.shape[0] // peers
        out = lax.all_to_all(rows.reshape(peers, per, D), "expert", split_axis=0, concat_axis=0, tiled=True)
        return out.reshape(peers * per, D)

    def pack(steps, where, rows, pieces):
        outs = (shape((slots * len(steps) // pieces, D), BF),) * pieces
        return call(functools.partial(pack_kernel, steps), outs, where, rows)

    def along(pieces, move):
        return [pieces[0]] + [
            lax.ppermute(pieces[d], "expert", [(i, move(i, d)) for i in range(peers)]) for d in range(1, len(pieces))
        ]

    def across_cores(pieces):
        return along(pieces, lambda i, d: i // NC * NC + (i + d) % NC)

    def along_z(pieces):
        return along(pieces, lambda i, d: (i // plane + d) % nz * plane + i % plane)

    def along_y(pieces):
        return along(pieces, lambda i, d: i // plane * plane + (i // NC + d) % NY * NC + i % NC)

    def mix(pieces, place):
        outs = (shape((slots // nz, D), BF),) * nz
        start = place * slots // NC
        return call(functools.partial(mix_kernel, start), outs, *pieces)

    def turn(pieces):
        outs = (shape((slots // NY, D), BF),) * NY
        return call(functools.partial(turn_kernel, len(pieces)), outs, *pieces)

    per_exp = peers * MOST
    x_shapes = tuple(shape((exp_dev, per_exp, n), BF) for n in (D, H, H, H))
    x_scratch = [pltpu.VMEM(s.shape, s.dtype) for s in x_shapes]
    x_scratch += [pltpu.VMEM(weight_in.shape, BF), pltpu.SemaphoreType.DMA((16,))]
    x_scratch += [pltpu.VMEM((peers, per_dev, D), F32)]

    def x_half(chunks, where):
        kernel = functools.partial(x_kernel, len(chunks))
        spaces = "s" + "v" * len(chunks) + "h"
        args = (where, *chunks, weight_in)
        return call(kernel, x_shapes, *args, spaces=spaces, out_spaces="hhhh", scratch=x_scratch)

    def g_half(g_in, silu, slope, keep):
        outs = (
            shape((exp_dev, per_exp, D), BF),
            shape((exp_dev, per_exp, 2 * H), BF),
            shape((slots, D), BF),
        )
        own = [] if keep else list(outs[:2])
        scratch = [pltpu.VMEM(s.shape, s.dtype) for s in own + [silu, slope, weight_in, weight_out]]
        scratch += [pltpu.VMEM((exp_dev, per_exp, D), F32), pltpu.VMEM((slots, D), BF), pltpu.SemaphoreType.DMA((24,))]
        kernel = functools.partial(g_kernel, keep)
        out_spaces = "vvh" if keep else "hhh"
        args = (g_in, silu, slope, weight_in, weight_out)
        return call(kernel, outs, *args, spaces="vhhhh", out_spaces=out_spaces, scratch=scratch)

    def home(step, send, back, gradient):
        outs = (shape((tokens, D), BF),)
        scratch = [pltpu.VMEM((tokens, D), BF), pltpu.VMEM((tokens, D), BF)]
        if send:
            outs += (shape((slots, D), BF),)
            scratch.append(pltpu.VMEM((slots, D), BF))
        scratch.append(pltpu.SemaphoreType.DMA((8,)))
        kernel = functools.partial(home_kernel, step, send)
        args = (place, column, back, gradient)
        return call(kernel, outs, *args, spaces="vvvh", out_spaces="h" * len(outs), scratch=scratch)

    def tick(value):
        return call(tick_kernel, (shape(value.shape, value.dtype),), value)[0]

    rows = D // dp + H // dp

    def after(values, *first):
        return lax.optimization_barrier((values, first))[0]

    saved = [None] * STEPS
    (x_pack,) = pack((2,), place, saved_inputs[2], 1)
    x_in = swap(x_pack)
    (g_pack,) = pack((2,), place, cotangent, 1)
    packed = pack((1, 0), place_near, saved_inputs, NC)
    packed = across_cores(packed)
    pieces = {}
    for k in (1, 0):
        pieces[k] = mix(packed, 1 - k)
    chunks, where = [x_in], sources
    gradient = cotangent
    for step in (2, 1, 0):
        g_in = swap(g_pack)
        x_rows, silu, slope, hidden = x_half(chunks, where)
        if step > 0:
            start = after(pieces[step - 1], hidden)
            got = along_z(start)
        if step == 1:
            column = tick(column)
        g_rows, pre, out = g_half(g_in, silu, slope, step == 0)
        saved[step] = (x_rows, pre, hidden, g_rows)
        if step > 0:
            returned = swap(out)
            got = after(got, out)
            turned_parts = turn(got)
            chunks, where = along_y(turned_parts), block_of
            column = tick(column)
            gradient, g_pack = home(step, True, returned, gradient)

    ahead = [(i, (i + 1) % dp) for i in range(dp)]
    behind = [(i, (i - 1) % dp) for i in range(dp)]

    def parts(picks, adds=(), dtype=BF):
        outs = (shape((rows, D), dtype),) * len(picks)
        kernel = functools.partial(grad_kernel, picks, dp)
        args = [one for step in saved for one in step] + list(adds)
        return call(kernel, outs, turns, *args, spaces="s" + "v" * len(args))

    def move(rows, way):
        return lax.ppermute(rows, "dp", way)

    far = parts(((0, 2), (1, 2)))
    far0 = move(far[0], ahead)
    far1 = move(far[1], behind)
    near = parts(((1, 1), (0, 3)))
    near1 = move(near[0], ahead)
    near0 = move(near[1], behind)
    returned = swap(out)
    last = parts(((0, 1), (1, 3)), (far0, far1))
    last0 = move(last[0], ahead)
    last1 = move(last[1], behind)
    own = parts(((0, 0), (1, 0)), dtype=F32)
    (gradient,) = home(0, False, returned, gradient)
    outs = (shape((exp_dev, D // dp, D), F32), shape((exp_dev, H // dp, D), F32))
    args = (own[0], near0, last0, own[1], near1, last1)
    win_grad, wout_grad = call(functools.partial(final_kernel, 3), outs, *args)
    return (gradient, win_grad, wout_grad)


def solution(mesh):
    in_specs = (
        P(None, ("dp", "expert"), None),
        P(("dp", "expert"), None),
        P("expert", None, None),
        P("expert", None, None),
        P(None, ("dp", "expert"), None),
    )
    out_specs = (P(("dp", "expert"), None), P("expert", "dp", None), P("expert", "dp", None))
    return jax.shard_map(program, mesh=mesh, in_specs=in_specs, out_specs=out_specs, check_vma=False)
```

profile of v0, /device:TPU:32, one launch (start us, length us, event | category | flops | bytes accessed | tf_op | source)
XLA Modules:
  0.0 429.9 jit_solution(8910876544443003404)
XLA Ops:
  4.4 11.8 %all-to-all-start.1 = ((bf16[64,8,1024]{2,1,0:T(8,128)(2,1)}), bf16[64,8,1024]{2,1,0:T(8,128)(2,1)S(1)}, u32[]{:S(2)}, u32[]{:S(2)}) async-start(bf16[64,8,1024]{2,1,0:T(8,128)(2,1)} %bitcast.6), calls=%async_computation.1 | async-start | bytes 2097152 | tf_op jit(solution)/shard_map/all_to_all | solution.py:391
  17.8 26.3 %all-to-all-done.1 = bf16[64,8,1024]{2,1,0:T(8,128)(2,1)S(1)} async-done(((bf16[64,8,1024]{2,1,0:T(8,128)(2,1)}), bf16[64,8,1024]{2,1,0:T(8,128)(2,1)S(1)}, u32[]{:S(2)}, u32[]{:S(2)}) %all-to-all-start.1) | async-done | bytes 1048608 | tf_op jit(solution)/shard_map/all_to_all | solution.py:391
  44.1 6.5 %all-to-all-start = ((bf16[64,8,1024]{2,1,0:T(8,128)(2,1)}), bf16[64,8,1024]{2,1,0:T(8,128)(2,1)S(1)}, u32[]{:S(2)}, u32[]{:S(2)}) async-start(bf16[64,8,1024]{2,1,0:T(8,128)(2,1)} %bitcast.3), calls=%async_computation | async-start | bytes 2097152 | tf_op jit(solution)/shard_map/all_to_all | solution.py:391
  50.7 8.5 %shard_map.81 = (bf16[2,256,1024]{2,1,0:T(8,128)(2,1)}, bf16[2,256,512]{2,1,0:T(8,128)(2,1)}, bf16[2,256,512]{2,1,0:T(8,128)(2,1)}, bf16[2,256,512]{2,1,0:T(8,128)(2,1)}) custom-call(s32[64]{0:T(128)S(1)} %iota.24.where_ref, bf16[512,1024]{1,0:T(8,128)(2,1)S(1)} %bitcast.34, bf16[2,1024,1024]{2,1,0:T(8,128)(2,1)} %win_hbm.5), custom_call_target="tpu_custom_call" | custom-call | tf_op jit(solution)/shard_map/pallas_call | solution.py:30
  59.1 19.4 %all-to-all-done = bf16[64,8,1024]{2,1,0:T(8,128)(2,1)S(1)} async-done(((bf16[64,8,1024]{2,1,0:T(8,128)(2,1)}), bf16[64,8,1024]{2,1,0:T(8,128)(2,1)S(1)}, u32[]{:S(2)}, u32[]{:S(2)}) %all-to-all-start) | async-done | bytes 1048608 | tf_op jit(solution)/shard_map/all_to_all | solution.py:391
  78.6 7.9 %shard_map.82 = (bf16[2,256,1024]{2,1,0:T(8,128)(2,1)}, bf16[2,256,1024]{2,1,0:T(8,128)(2,1)}, bf16[512,1024]{1,0:T(8,128)(2,1)}) custom-call(bf16[512,1024]{1,0:T(8,128)(2,1)S(1)} %bitcast.37, bf16[2,256,512]{2,1,0:T(8,128)(2,1)} %get-tuple-element.96.silu_hbm, bf16[2,256,512]{2,1,0:T(8,128)(2,1)} %get-tuple-element.97.slope_hbm, ...), custom_call_target="tpu_custom_call" | custom-call | tf_op jit(solution)/shard_map/pallas_call | solution.py:30
  86.5 6.6 %all-to-all-start.2 = ((bf16[64,8,1024]{2,1,0:T(8,128)(2,1)}), bf16[64,8,1024]{2,1,0:T(8,128)(2,1)S(1)}, u32[]{:S(2)}, u32[]{:S(2)}) async-start(bf16[64,8,1024]{2,1,0:T(8,128)(2,1)} %bitcast.43), calls=%async_computation.2 | async-start | bytes 2097152 | tf_op jit(solution)/shard_map/all_to_all | solution.py:391
  93.2 27.7 %all-to-all-done.2 = bf16[64,8,1024]{2,1,0:T(8,128)(2,1)S(1)} async-done(((bf16[64,8,1024]{2,1,0:T(8,128)(2,1)}), bf16[64,8,1024]{2,1,0:T(8,128)(2,1)S(1)}, u32[]{:S(2)}, u32[]{:S(2)}) %all-to-all-start.2) | async-done | bytes 1048608 | tf_op jit(solution)/shard_map/all_to_all | solution.py:391
  121.0 4.7 %shard_map.83 = (bf16[256,1024]{1,0:T(8,128)(2,1)}, bf16[512,1024]{1,0:T(8,128)(2,1)}) custom-call(s32[3,256]{1,0:T(4,128)S(1)} %get-tuple-element.190.row_ref, s32[256,3]{1,0:T(8,128)S(1)} %shard_map.76.ref.col_ref, bf16[512,1024]{1,0:T(8,128)(2,1)S(1)} %bitcast.33, bf16[256,1024]{1,0:T(8,128)(2,1)} %g_hbm.1), custom_call_target="tpu_custom_call" | custom-call | tf_op jit(solution)/shard_map/pallas_call | solution.py:30
  125.7 6.5 %all-to-all-start.3 = ((bf16[64,8,1024]{2,1,0:T(8,128)(2,1)}), bf16[64,8,1024]{2,1,0:T(8,128)(2,1)S(1)}, u32[]{:S(2)}, u32[]{:S(2)}) async-start(bf16[64,8,1024]{2,1,0:T(8,128)(2,1)} %bitcast.39), calls=%async_computation.3 | async-start | bytes 2097152 | tf_op jit(solution)/shard_map/all_to_all | solution.py:391
  148.3 10.9 %collective-permute-done.1.refs_1_ = bf16[64,1024]{1,0:T(8,128)(2,1)S(1)} collective-permute-done((bf16[64,1024]{1,0:T(8,128)(2,1)S(1)}, bf16[64,1024]{1,0:T(8,128)(2,1)S(1)}, u32[]{:S(2)}, u32[]{:S(2)}) %collective-permute-start.1) | collective-permute-done | bytes 131104 | tf_op jit(solution)/shard_map/ppermute | solution.py:400
  159.2 4.3 %collective-permute-start.6 = (bf16[64,1024]{1,0:T(8,128)(2,1)S(1)}, bf16[64,1024]{1,0:T(8,128)(2,1)S(1)}, u32[]{:S(2)}, u32[]{:S(2)}) collective-permute-start(bf16[64,1024]{1,0:T(8,128)(2,1)S(1)} %get-tuple-element.117), channel_id=1, source_target_pairs={{0,48},{1,49},{2,50},{3,51},{4,52},{5,53},{6,54},{7,55},{8,56},{9,... | collective-permute-start | bytes 393224 | tf_op jit(solution)/shard_map/ppermute | solution.py:400
  163.5 4.6 %collective-permute-done.2.refs_2_ = bf16[64,1024]{1,0:T(8,128)(2,1)S(1)} collective-permute-done((bf16[64,1024]{1,0:T(8,128)(2,1)S(1)}, bf16[64,1024]{1,0:T(8,128)(2,1)S(1)}, u32[]{:S(2)}, u32[]{:S(2)}) %collective-permute-start.2) | collective-permute-done | bytes 131104 | tf_op jit(solution)/shard_map/ppermute | solution.py:400
  189.0 6.1 %collective-permute-done.9.refs_2_ = bf16[128,1024]{1,0:T(8,128)(2,1)S(1)} collective-permute-done((bf16[128,1024]{1,0:T(8,128)(2,1)S(1)}, bf16[128,1024]{1,0:T(8,128)(2,1)S(1)}, u32[]{:S(2)}, u32[]{:S(2)}) %collective-permute-start.9) | collective-permute-done | bytes 262176 | tf_op jit(solution)/shard_map/ppermute | solution.py:400
  195.1 8.5 %shard_map.87 = (bf16[2,256,1024]{2,1,0:T(8,128)(2,1)}, bf16[2,256,512]{2,1,0:T(8,128)(2,1)}, bf16[2,256,512]{2,1,0:T(8,128)(2,1)}, bf16[2,256,512]{2,1,0:T(8,128)(2,1)}) custom-call(s32[64]{0:T(128)S(1)} %fusion.24.where_ref, bf16[128,1024]{1,0:T(8,128)(2,1)S(1)} %get-tuple-element.127.refs_0_, bf16[128,1024]{1,0:T(8,128)(2,1)S(1)} %collective-permute-done.8.refs_1_, ...), custom_call_target="tpu_custom_call" | custom-call | tf_op jit(solution)/shard_map/pallas_call | solution.py:30
  203.6 7.9 %shard_map.88 = (bf16[2,256,1024]{2,1,0:T(8,128)(2,1)}, bf16[2,256,1024]{2,1,0:T(8,128)(2,1)}, bf16[512,1024]{1,0:T(8,128)(2,1)}) custom-call(bf16[512,1024]{1,0:T(8,128)(2,1)S(1)} %bitcast.35, bf16[2,256,512]{2,1,0:T(8,128)(2,1)} %get-tuple-element.131.silu_hbm, bf16[2,256,512]{2,1,0:T(8,128)(2,1)} %get-tuple-element.132.slope_hbm, ...), custom_call_target="tpu_custom_call" | custom-call | tf_op jit(solution)/shard_map/pallas_call | solution.py:30
  211.6 9.3 %all-to-all-start.4 = ((bf16[64,8,1024]{2,1,0:T(8,128)(2,1)}), bf16[64,8,1024]{2,1,0:T(8,128)(2,1)S(1)}, u32[]{:S(2)}, u32[]{:S(2)}) async-start(bf16[64,8,1024]{2,1,0:T(8,128)(2,1)} %bitcast.42), calls=%async_computation.4 | async-start | bytes 2097152 | tf_op jit(solution)/shard_map/all_to_all | solution.py:391
  220.9 27.9 %all-to-all-done.4 = bf16[64,8,1024]{2,1,0:T(8,128)(2,1)S(1)} async-done(((bf16[64,8,1024]{2,1,0:T(8,128)(2,1)}), bf16[64,8,1024]{2,1,0:T(8,128)(2,1)S(1)}, u32[]{:S(2)}, u32[]{:S(2)}) %all-to-all-start.4) | async-done | bytes 1048608 | tf_op jit(solution)/shard_map/all_to_all | solution.py:391
  248.8 4.7 %shard_map.89 = (bf16[256,1024]{1,0:T(8,128)(2,1)}, bf16[512,1024]{1,0:T(8,128)(2,1)}) custom-call(s32[3,256]{1,0:T(4,128)S(1)} %get-tuple-element.190.row_ref, s32[256,3]{1,0:T(8,128)S(1)} %shard_map.78.col_ref, bf16[512,1024]{1,0:T(8,128)(2,1)S(1)} %bitcast.32, bf16[256,1024]{1,0:T(8,128)(2,1)} %get-tuple-element.134.g_hbm), custom_call_target="tpu_custom_call" | custom-call | tf_op jit(solution)/shard_map/pallas_call | solution.py:30
  253.5 6.5 %all-to-all-start.5 = ((bf16[64,8,1024]{2,1,0:T(8,128)(2,1)}), bf16[64,8,1024]{2,1,0:T(8,128)(2,1)S(1)}, u32[]{:S(2)}, u32[]{:S(2)}) async-start(bf16[64,8,1024]{2,1,0:T(8,128)(2,1)} %bitcast.40), calls=%async_computation.5 | async-start | bytes 2097152 | tf_op jit(solution)/shard_map/all_to_all | solution.py:391
  270.7 16.3 %collective-permute-done.11.refs_1_ = bf16[64,1024]{1,0:T(8,128)(2,1)S(1)} collective-permute-done((bf16[64,1024]{1,0:T(8,128)(2,1)S(1)}, bf16[64,1024]{1,0:T(8,128)(2,1)S(1)}, u32[]{:S(2)}, u32[]{:S(2)}) %collective-permute-start.11) | collective-permute-done | bytes 131104 | tf_op jit(solution)/shard_map/ppermute | solution.py:400
  287.0 4.3 %collective-permute-start.16 = (bf16[64,1024]{1,0:T(8,128)(2,1)S(1)}, bf16[64,1024]{1,0:T(8,128)(2,1)S(1)}, u32[]{:S(2)}, u32[]{:S(2)}) collective-permute-start(bf16[64,1024]{1,0:T(8,128)(2,1)S(1)} %get-tuple-element.151), channel_id=1, source_target_pairs={{0,48},{1,49},{2,50},{3,51},{4,52},{5,53},{6,54},{7,55},{8,56},{9,... | collective-permute-start | bytes 393224 | tf_op jit(solution)/shard_map/ppermute | solution.py:400
  291.4 4.6 %collective-permute-done.12.refs_2_ = bf16[64,1024]{1,0:T(8,128)(2,1)S(1)} collective-permute-done((bf16[64,1024]{1,0:T(8,128)(2,1)S(1)}, bf16[64,1024]{1,0:T(8,128)(2,1)S(1)}, u32[]{:S(2)}, u32[]{:S(2)}) %collective-permute-start.12) | collective-permute-done | bytes 131104 | tf_op jit(solution)/shard_map/ppermute | solution.py:400
  316.9 6.1 %collective-permute-done.19.refs_2_ = bf16[128,1024]{1,0:T(8,128)(2,1)S(1)} collective-permute-done((bf16[128,1024]{1,0:T(8,128)(2,1)S(1)}, bf16[128,1024]{1,0:T(8,128)(2,1)S(1)}, u32[]{:S(2)}, u32[]{:S(2)}) %collective-permute-start.19) | collective-permute-done | bytes 262176 | tf_op jit(solution)/shard_map/ppermute | solution.py:400
  323.0 8.5 %shard_map.92 = (bf16[2,256,1024]{2,1,0:T(8,128)(2,1)}, bf16[2,256,512]{2,1,0:T(8,128)(2,1)}, bf16[2,256,512]{2,1,0:T(8,128)(2,1)}, bf16[2,256,512]{2,1,0:T(8,128)(2,1)}) custom-call(s32[64]{0:T(128)S(1)} %fusion.24.where_ref, bf16[128,1024]{1,0:T(8,128)(2,1)S(1)} %get-tuple-element.161.refs_0_, bf16[128,1024]{1,0:T(8,128)(2,1)S(1)} %collective-permute-done.18.refs_1_, ...), custom_call_target="tpu_custom_call" | custom-call | tf_op jit(solution)/shard_map/pallas_call | solution.py:30
  333.7 8.0 %shard_map.93 = (bf16[2,256,1024]{2,1,0:T(8,128)(2,1)S(1)}, bf16[2,256,1024]{2,1,0:T(8,128)(2,1)S(1)}, bf16[512,1024]{1,0:T(8,128)(2,1)}) custom-call(bf16[512,1024]{1,0:T(8,128)(2,1)S(1)} %bitcast.36, bf16[2,256,512]{2,1,0:T(8,128)(2,1)} %get-tuple-element.165.silu_hbm, bf16[2,256,512]{2,1,0:T(8,128)(2,1)} %get-tuple-element.166.slope_hbm, ...), custom_call_target="tpu_custom_call" | custom-call | tf_op jit(solution)/shard_map/pallas_call | solution.py:30
  343.7 9.6 %all-to-all-start.6 = ((bf16[64,8,1024]{2,1,0:T(8,128)(2,1)}), bf16[64,8,1024]{2,1,0:T(8,128)(2,1)}, u32[]{:S(2)}, u32[]{:S(2)}) async-start(bf16[64,8,1024]{2,1,0:T(8,128)(2,1)} %bitcast.41), calls=%async_computation.6 | async-start | bytes 2097152 | tf_op jit(solution)/shard_map/all_to_all | solution.py:391
  377.4 12.2 %collective-permute-done.22.refs_12_ = bf16[384,1024]{1,0:T(8,128)(2,1)S(1)} collective-permute-done((bf16[384,1024]{1,0:T(8,128)(2,1)S(1)}, bf16[384,1024]{1,0:T(8,128)(2,1)S(1)}, u32[]{:S(2)}, u32[]{:S(2)}) %collective-permute-start.22) | collective-permute-done | bytes 786464 | tf_op jit(solution)/shard_map/ppermute | solution.py:505
  389.9 4.2 shard_map.98
  401.4 5.4 %collective-permute-done.21.refs_1_ = bf16[384,1024]{1,0:T(8,128)(2,1)S(1)} collective-permute-done((bf16[384,1024]{1,0:T(8,128)(2,1)S(1)}, bf16[384,1024]{1,0:T(8,128)(2,1)S(1)}, u32[]{:S(2)}, u32[]{:S(2)}) %collective-permute-start.21) | collective-permute-done | bytes 786464 | tf_op jit(solution)/shard_map/ppermute | solution.py:505
  406.7 15.7 %collective-permute-done.24.refs_2_ = bf16[384,1024]{1,0:T(8,128)(2,1)S(1)} collective-permute-done((bf16[384,1024]{1,0:T(8,128)(2,1)S(1)}, bf16[384,1024]{1,0:T(8,128)(2,1)S(1)}, u32[]{:S(2)}, u32[]{:S(2)}) %collective-permute-start.24) | collective-permute-done | bytes 786464 | tf_op jit(solution)/shard_map/ppermute | solution.py:505
  424.7 5.1 %shard_map.94 = bf16[256,1024]{1,0:T(8,128)(2,1)} custom-call(s32[3,256]{1,0:T(4,128)S(1)} %get-tuple-element.190.row_ref, s32[256,3]{1,0:T(8,128)S(1)} %shard_map.78.col_ref, bf16[512,1024]{1,0:T(8,128)(2,1)} %bitcast.17.back_ref, bf16[256,1024]{1,0:T(8,128)(2,1)} %get-tuple-element.168.g_hbm), custom_call_target="tpu_custom_call" | custom-call | tf_op jit(solution)/shard_map/pallas_call | solution.py:30
  (106 shorter events, 112.1 us)
Async XLA Ops:
  4.4 39.7 %all-to-all-start.1 = ((bf16[64,8,1024]{2,1,0:T(8,128)(2,1)}), bf16[64,8,1024]{2,1,0:T(8,128)(2,1)S(1)}, u32[]{:S(2)}, u32[]{:S(2)}) async-start(bf16[64,8,1024]{2,1,0:T(8,128)(2,1)} %bitcast.6), calls=%async_computation.1 | async-start | bytes 2097152 | tf_op jit(solution)/shard_map/all_to_all | solution.py:391
  44.1 34.4 %all-to-all-start = ((bf16[64,8,1024]{2,1,0:T(8,128)(2,1)}), bf16[64,8,1024]{2,1,0:T(8,128)(2,1)S(1)}, u32[]{:S(2)}, u32[]{:S(2)}) async-start(bf16[64,8,1024]{2,1,0:T(8,128)(2,1)} %bitcast.3), calls=%async_computation | async-start | bytes 2097152 | tf_op jit(solution)/shard_map/all_to_all | solution.py:391
  86.5 34.5 %all-to-all-start.2 = ((bf16[64,8,1024]{2,1,0:T(8,128)(2,1)}), bf16[64,8,1024]{2,1,0:T(8,128)(2,1)S(1)}, u32[]{:S(2)}, u32[]{:S(2)}) async-start(bf16[64,8,1024]{2,1,0:T(8,128)(2,1)} %bitcast.43), calls=%async_computation.2 | async-start | bytes 2097152 | tf_op jit(solution)/shard_map/all_to_all | solution.py:391
  125.7 77.9 %all-to-all-start.3 = ((bf16[64,8,1024]{2,1,0:T(8,128)(2,1)}), bf16[64,8,1024]{2,1,0:T(8,128)(2,1)S(1)}, u32[]{:S(2)}, u32[]{:S(2)}) async-start(bf16[64,8,1024]{2,1,0:T(8,128)(2,1)} %bitcast.39), calls=%async_computation.3 | async-start | bytes 2097152 | tf_op jit(solution)/shard_map/all_to_all | solution.py:391
  137.7 21.5 %collective-permute-start.1 = (bf16[64,1024]{1,0:T(8,128)(2,1)S(1)}, bf16[64,1024]{1,0:T(8,128)(2,1)S(1)}, u32[]{:S(2)}, u32[]{:S(2)}) collective-permute-start(bf16[64,1024]{1,0:T(8,128)(2,1)S(1)} %get-tuple-element.112), channel_id=1, source_target_pairs={{0,8},{1,9},{2,10},{3,11},{4,12},{5,13},{6,14},{7,15},{8,16},{9,17... | collective-permute-start | bytes 393224 | tf_op jit(solution)/shard_map/ppermute | solution.py:400
  139.2 28.9 %collective-permute-start.2 = (bf16[64,1024]{1,0:T(8,128)(2,1)S(1)}, bf16[64,1024]{1,0:T(8,128)(2,1)S(1)}, u32[]{:S(2)}, u32[]{:S(2)}) collective-permute-start(bf16[64,1024]{1,0:T(8,128)(2,1)S(1)} %get-tuple-element.113), channel_id=1, source_target_pairs={{0,16},{1,17},{2,18},{3,19},{4,20},{5,21},{6,22},{7,23},{8,24},{9,... | collective-permute-start | bytes 393224 | tf_op jit(solution)/shard_map/ppermute | solution.py:400
  142.9 30.1 %collective-permute-start.3 = (bf16[64,1024]{1,0:T(8,128)(2,1)S(1)}, bf16[64,1024]{1,0:T(8,128)(2,1)S(1)}, u32[]{:S(2)}, u32[]{:S(2)}) collective-permute-start(bf16[64,1024]{1,0:T(8,128)(2,1)S(1)} %get-tuple-element.114), channel_id=1, source_target_pairs={{0,24},{1,25},{2,26},{3,27},{4,28},{5,29},{6,30},{7,31},{8,32},{9,... | collective-permute-start | bytes 393224 | tf_op jit(solution)/shard_map/ppermute | solution.py:400
  143.6 29.4 %collective-permute-start.4 = (bf16[64,1024]{1,0:T(8,128)(2,1)S(1)}, bf16[64,1024]{1,0:T(8,128)(2,1)S(1)}, u32[]{:S(2)}, u32[]{:S(2)}) collective-permute-start(bf16[64,1024]{1,0:T(8,128)(2,1)S(1)} %get-tuple-element.115), channel_id=1, source_target_pairs={{0,32},{1,33},{2,34},{3,35},{4,36},{5,37},{6,38},{7,39},{8,40},{9,... | collective-permute-start | bytes 393224 | tf_op jit(solution)/shard_map/ppermute | solution.py:400
  146.7 27.7 %collective-permute-start.5 = (bf16[64,1024]{1,0:T(8,128)(2,1)S(1)}, bf16[64,1024]{1,0:T(8,128)(2,1)S(1)}, u32[]{:S(2)}, u32[]{:S(2)}) collective-permute-start(bf16[64,1024]{1,0:T(8,128)(2,1)S(1)} %get-tuple-element.116), channel_id=1, source_target_pairs={{0,40},{1,41},{2,42},{3,43},{4,44},{5,45},{6,46},{7,47},{8,48},{9,... | collective-permute-start | bytes 393224 | tf_op jit(solution)/shard_map/ppermute | solution.py:400
  159.2 18.0 %collective-permute-start.6 = (bf16[64,1024]{1,0:T(8,128)(2,1)S(1)}, bf16[64,1024]{1,0:T(8,128)(2,1)S(1)}, u32[]{:S(2)}, u32[]{:S(2)}) collective-permute-start(bf16[64,1024]{1,0:T(8,128)(2,1)S(1)} %get-tuple-element.117), channel_id=1, source_target_pairs={{0,48},{1,49},{2,50},{3,51},{4,52},{5,53},{6,54},{7,55},{8,56},{9,... | collective-permute-start | bytes 393224 | tf_op jit(solution)/shard_map/ppermute | solution.py:400
  168.1 11.3 %collective-permute-start.7 = (bf16[64,1024]{1,0:T(8,128)(2,1)S(1)}, bf16[64,1024]{1,0:T(8,128)(2,1)S(1)}, u32[]{:S(2)}, u32[]{:S(2)}) collective-permute-start(bf16[64,1024]{1,0:T(8,128)(2,1)S(1)} %get-tuple-element.118), channel_id=1, source_target_pairs={{0,56},{1,57},{2,58},{3,59},{4,60},{5,61},{6,62},{7,63},{8,0},{9,1... | collective-permute-start | bytes 393224 | tf_op jit(solution)/shard_map/ppermute | solution.py:400
  179.5 9.5 %collective-permute-start.8 = (bf16[128,1024]{1,0:T(8,128)(2,1)S(1)}, bf16[128,1024]{1,0:T(8,128)(2,1)S(1)}, u32[]{:S(2)}, u32[]{:S(2)}) collective-permute-start(bf16[128,1024]{1,0:T(8,128)(2,1)S(1)} %get-tuple-element.128), channel_id=1, source_target_pairs={{0,2},{1,3},{2,4},{3,5},{4,6},{5,7},{6,0},{7,1},{8,10},{9,11},{10,... | collective-permute-start | bytes 786440 | tf_op jit(solution)/shard_map/ppermute | solution.py:400
  181.1 14.1 %collective-permute-start.9 = (bf16[128,1024]{1,0:T(8,128)(2,1)S(1)}, bf16[128,1024]{1,0:T(8,128)(2,1)S(1)}, u32[]{:S(2)}, u32[]{:S(2)}) collective-permute-start(bf16[128,1024]{1,0:T(8,128)(2,1)S(1)} %get-tuple-element.129), channel_id=1, source_target_pairs={{0,4},{1,5},{2,6},{3,7},{4,0},{5,1},{6,2},{7,3},{8,12},{9,13},{10,... | collective-permute-start | bytes 786440 | tf_op jit(solution)/shard_map/ppermute | solution.py:400
  183.8 11.3 %collective-permute-start.10 = (bf16[128,1024]{1,0:T(8,128)(2,1)S(1)}, bf16[128,1024]{1,0:T(8,128)(2,1)S(1)}, u32[]{:S(2)}, u32[]{:S(2)}) collective-permute-start(bf16[128,1024]{1,0:T(8,128)(2,1)S(1)} %get-tuple-element.130), channel_id=1, source_target_pairs={{0,6},{1,7},{2,0},{3,1},{4,2},{5,3},{6,4},{7,5},{8,14},{9,15},{10,... | collective-permute-start | bytes 786440 | tf_op jit(solution)/shard_map/ppermute | solution.py:400
  211.6 37.3 %all-to-all-start.4 = ((bf16[64,8,1024]{2,1,0:T(8,128)(2,1)}), bf16[64,8,1024]{2,1,0:T(8,128)(2,1)S(1)}, u32[]{:S(2)}, u32[]{:S(2)}) async-start(bf16[64,8,1024]{2,1,0:T(8,128)(2,1)} %bitcast.42), calls=%async_computation.4 | async-start | bytes 2097152 | tf_op jit(solution)/shard_map/all_to_all | solution.py:391
  253.5 77.9 %all-to-all-start.5 = ((bf16[64,8,1024]{2,1,0:T(8,128)(2,1)}), bf16[64,8,1024]{2,1,0:T(8,128)(2,1)S(1)}, u32[]{:S(2)}, u32[]{:S(2)}) async-start(bf16[64,8,1024]{2,1,0:T(8,128)(2,1)} %bitcast.40), calls=%async_computation.5 | async-start | bytes 2097152 | tf_op jit(solution)/shard_map/all_to_all | solution.py:391
  260.1 26.9 %collective-permute-start.11 = (bf16[64,1024]{1,0:T(8,128)(2,1)S(1)}, bf16[64,1024]{1,0:T(8,128)(2,1)S(1)}, u32[]{:S(2)}, u32[]{:S(2)}) collective-permute-start(bf16[64,1024]{1,0:T(8,128)(2,1)S(1)} %get-tuple-element.146), channel_id=1, source_target_pairs={{0,8},{1,9},{2,10},{3,11},{4,12},{5,13},{6,14},{7,15},{8,16},{9,17... | collective-permute-start | bytes 393224 | tf_op jit(solution)/shard_map/ppermute | solution.py:400
  261.7 34.2 %collective-permute-start.12 = (bf16[64,1024]{1,0:T(8,128)(2,1)S(1)}, bf16[64,1024]{1,0:T(8,128)(2,1)S(1)}, u32[]{:S(2)}, u32[]{:S(2)}) collective-permute-start(bf16[64,1024]{1,0:T(8,128)(2,1)S(1)} %get-tuple-element.147), channel_id=1, source_target_pairs={{0,16},{1,17},{2,18},{3,19},{4,20},{5,21},{6,22},{7,23},{8,24},{9,... | collective-permute-start | bytes 393224 | tf_op jit(solution)/shard_map/ppermute | solution.py:400
  265.4 35.5 %collective-permute-start.13 = (bf16[64,1024]{1,0:T(8,128)(2,1)S(1)}, bf16[64,1024]{1,0:T(8,128)(2,1)S(1)}, u32[]{:S(2)}, u32[]{:S(2)}) collective-permute-start(bf16[64,1024]{1,0:T(8,128)(2,1)S(1)} %get-tuple-element.148), channel_id=1, source_target_pairs={{0,24},{1,25},{2,26},{3,27},{4,28},{5,29},{6,30},{7,31},{8,32},{9,... | collective-permute-start | bytes 393224 | tf_op jit(solution)/shard_map/ppermute | solution.py:400
  266.1 34.8 %collective-permute-start.14 = (bf16[64,1024]{1,0:T(8,128)(2,1)S(1)}, bf16[64,1024]{1,0:T(8,128)(2,1)S(1)}, u32[]{:S(2)}, u32[]{:S(2)}) collective-permute-start(bf16[64,1024]{1,0:T(8,128)(2,1)S(1)} %get-tuple-element.149), channel_id=1, source_target_pairs={{0,32},{1,33},{2,34},{3,35},{4,36},{5,37},{6,38},{7,39},{8,40},{9,... | collective-permute-start | bytes 393224 | tf_op jit(solution)/shard_map/ppermute | solution.py:400
  269.1 33.0 %collective-permute-start.15 = (bf16[64,1024]{1,0:T(8,128)(2,1)S(1)}, bf16[64,1024]{1,0:T(8,128)(2,1)S(1)}, u32[]{:S(2)}, u32[]{:S(2)}) collective-permute-start(bf16[64,1024]{1,0:T(8,128)(2,1)S(1)} %get-tuple-element.150), channel_id=1, source_target_pairs={{0,40},{1,41},{2,42},{3,43},{4,44},{5,45},{6,46},{7,47},{8,48},{9,... | collective-permute-start | bytes 393224 | tf_op jit(solution)/shard_map/ppermute | solution.py:400
  287.0 18.0 %collective-permute-start.16 = (bf16[64,1024]{1,0:T(8,128)(2,1)S(1)}, bf16[64,1024]{1,0:T(8,128)(2,1)S(1)}, u32[]{:S(2)}, u32[]{:S(2)}) collective-permute-start(bf16[64,1024]{1,0:T(8,128)(2,1)S(1)} %get-tuple-element.151), channel_id=1, source_target_pairs={{0,48},{1,49},{2,50},{3,51},{4,52},{5,53},{6,54},{7,55},{8,56},{9,... | collective-permute-start | bytes 393224 | tf_op jit(solution)/shard_map/ppermute | solution.py:400
  295.9 11.3 %collective-permute-start.17 = (bf16[64,1024]{1,0:T(8,128)(2,1)S(1)}, bf16[64,1024]{1,0:T(8,128)(2,1)S(1)}, u32[]{:S(2)}, u32[]{:S(2)}) collective-permute-start(bf16[64,1024]{1,0:T(8,128)(2,1)S(1)} %get-tuple-element.152), channel_id=1, source_target_pairs={{0,56},{1,57},{2,58},{3,59},{4,60},{5,61},{6,62},{7,63},{8,0},{9,1... | collective-permute-start | bytes 393224 | tf_op jit(solution)/shard_map/ppermute | solution.py:400
  308.9 14.1 %collective-permute-start.19 = (bf16[128,1024]{1,0:T(8,128)(2,1)S(1)}, bf16[128,1024]{1,0:T(8,128)(2,1)S(1)}, u32[]{:S(2)}, u32[]{:S(2)}) collective-permute-start(bf16[128,1024]{1,0:T(8,128)(2,1)S(1)} %get-tuple-element.163), channel_id=1, source_target_pairs={{0,4},{1,5},{2,6},{3,7},{4,0},{5,1},{6,2},{7,3},{8,12},{9,13},{10,... | collective-permute-start | bytes 786440 | tf_op jit(solution)/shard_map/ppermute | solution.py:400
  311.6 11.3 %collective-permute-start.20 = (bf16[128,1024]{1,0:T(8,128)(2,1)S(1)}, bf16[128,1024]{1,0:T(8,128)(2,1)S(1)}, u32[]{:S(2)}, u32[]{:S(2)}) collective-permute-start(bf16[128,1024]{1,0:T(8,128)(2,1)S(1)} %get-tuple-element.164), channel_id=1, source_target_pairs={{0,6},{1,7},{2,0},{3,1},{4,2},{5,3},{6,4},{7,5},{8,14},{9,15},{10,... | collective-permute-start | bytes 786440 | tf_op jit(solution)/shard_map/ppermute | solution.py:400
  343.7 81.0 %all-to-all-start.6 = ((bf16[64,8,1024]{2,1,0:T(8,128)(2,1)}), bf16[64,8,1024]{2,1,0:T(8,128)(2,1)}, u32[]{:S(2)}, u32[]{:S(2)}) async-start(bf16[64,8,1024]{2,1,0:T(8,128)(2,1)} %bitcast.41), calls=%async_computation.6 | async-start | bytes 2097152 | tf_op jit(solution)/shard_map/all_to_all | solution.py:391
  367.9 21.7 %collective-permute-start.22 = (bf16[384,1024]{1,0:T(8,128)(2,1)S(1)}, bf16[384,1024]{1,0:T(8,128)(2,1)S(1)}, u32[]{:S(2)}, u32[]{:S(2)}) collective-permute-start(bf16[384,1024]{1,0:T(8,128)(2,1)S(1)} %get-tuple-element.181), channel_id=1, source_target_pairs={{0,64},{64,128},{128,192},{192,0},{1,65},{65,129},{129,193},{193,1... | collective-permute-start | bytes 2359304 | tf_op jit(solution)/shard_map/ppermute | solution.py:505
  369.5 20.4 %collective-permute-start.23 = (bf16[384,1024]{1,0:T(8,128)(2,1)S(1)}, bf16[384,1024]{1,0:T(8,128)(2,1)S(1)}, u32[]{:S(2)}, u32[]{:S(2)}) collective-permute-start(bf16[384,1024]{1,0:T(8,128)(2,1)S(1)} %get-tuple-element.182), channel_id=1, source_target_pairs={{0,192},{64,0},{128,64},{192,128},{1,193},{65,1},{129,65},{193,129... | collective-permute-start | bytes 2359304 | tf_op jit(solution)/shard_map/ppermute | solution.py:505
  375.3 31.5 %collective-permute-start.21 = (bf16[384,1024]{1,0:T(8,128)(2,1)S(1)}, bf16[384,1024]{1,0:T(8,128)(2,1)S(1)}, u32[]{:S(2)}, u32[]{:S(2)}) collective-permute-start(bf16[384,1024]{1,0:T(8,128)(2,1)S(1)} %get-tuple-element.180), channel_id=1, source_target_pairs={{0,192},{64,0},{128,64},{192,128},{1,193},{65,1},{129,65},{193,129... | collective-permute-start | bytes 2359304 | tf_op jit(solution)/shard_map/ppermute | solution.py:505
  376.9 29.9 %collective-permute-start.25 = (bf16[384,1024]{1,0:T(8,128)(2,1)S(1)}, bf16[384,1024]{1,0:T(8,128)(2,1)S(1)}, u32[]{:S(2)}, u32[]{:S(2)}) collective-permute-start(bf16[384,1024]{1,0:T(8,128)(2,1)S(1)} %get-tuple-element.185), channel_id=1, source_target_pairs={{0,64},{64,128},{128,192},{192,0},{1,65},{65,129},{129,193},{193,1... | collective-permute-start | bytes 2359304 | tf_op jit(solution)/shard_map/ppermute | solution.py:505
  394.1 28.3 %collective-permute-start.24 = (bf16[384,1024]{1,0:T(8,128)(2,1)S(1)}, bf16[384,1024]{1,0:T(8,128)(2,1)S(1)}, u32[]{:S(2)}, u32[]{:S(2)}) collective-permute-start(bf16[384,1024]{1,0:T(8,128)(2,1)S(1)} %get-tuple-element.183), channel_id=1, source_target_pairs={{0,64},{64,128},{128,192},{192,0},{1,65},{65,129},{129,193},{193,1... | collective-permute-start | bytes 2359304 | tf_op jit(solution)/shard_map/ppermute | solution.py:505
  395.6 26.9 %collective-permute-start.26 = (bf16[384,1024]{1,0:T(8,128)(2,1)S(1)}, bf16[384,1024]{1,0:T(8,128)(2,1)S(1)}, u32[]{:S(2)}, u32[]{:S(2)}) collective-permute-start(bf16[384,1024]{1,0:T(8,128)(2,1)S(1)} %get-tuple-element.186), channel_id=1, source_target_pairs={{0,192},{64,0},{128,64},{192,128},{1,193},{65,1},{129,65},{193,129... | collective-permute-start | bytes 2359304 | tf_op jit(solution)/shard_map/ppermute | solution.py:505
  (21 other events, 82.9 us)
where the time goes:
time: 432 us; the launch traced here: 430 us
  waiting for transfers between devices  213 us (49%)
  starting transfers between devices  111 us (26%)
  Pallas kernels  86.8 us (20%)
  local copies, waits for them, and re-layouts  18 us (4%)
    all_to_all x7, waiting for transfers between devices, swap(): lax.all_to_all(rows.reshape(peers, per, D), 'expert', split_axis=0, conca...  101 us
    pallas_call x24, Pallas kernels, call(): pl.pallas_call(kernel, out_shape=outs, in_specs=ins, out_specs=tuple((pl....  86.8 us
    ppermute x21, waiting for transfers between devices, along(): lax.ppermute(pieces[d], 'expert', [(i, move(i, d)) for i in range(peers)])  77.9 us
    all_to_all x7, starting transfers between devices, swap(): lax.all_to_all(rows.reshape(peers, per, D), 'expert', split_axis=0, conca...  56.9 us
    ppermute x21, starting transfers between devices, along(): lax.ppermute(pieces[d], 'expert', [(i, move(i, d)) for i in range(peers)])  45 us
    ppermute x6, waiting for transfers between devices, move(): return lax.ppermute(rows, 'dp', way)  33.6 us
    unnamed x39, local copies, waits for them, and re-layouts  16.8 us
    ppermute x6, starting transfers between devices, move(): return lax.ppermute(rows, 'dp', way)  8.73 us
  transfers between devices with their start and end apart: 34, of which 26 were waited for; matrix products, arithmetic and copies ran while one was open for 0% of the time, Pallas kernels for 11%

commit v1 on v0

--- a/solution.py
+++ b/solution.py
@@ -81,30 +81,46 @@
     return ids * MOST + rank
 
 
+def chosen(row, rows, start, count):
+    sel = lax.broadcasted_iota(jnp.int32, (count, row.shape[1]), 0) + start == row
+    return dot(sel.astype(BF), rows)
+
+
 def picked(row, rows, start, count):
-    sel = lax.broadcasted_iota(jnp.int32, (count, row.shape[1]), 0) + start == row
-    return dot(sel.astype(BF), rows).astype(BF)
-
-
-def pack_kernel(steps, row_ref, x_ref, *outs):
+    return chosen(row, rows, start, count).astype(BF)
+
+
+def pack_kernel(step, row_ref, x_ref, *outs):
     for n, out in enumerate(outs):
-        size = out.shape[0] // len(steps)
-        per = size // 256
+        size = out.shape[0]
 
         def part(i):
-            k = i // per
-            step = steps[0] - k
-            x = x_ref[step] if len(x_ref.shape) == 3 else x_ref[...]
-            out[block(i, 256)] = picked(row_ref[pl.ds(step, 1)], x, n * size + i % per * 256, 256)
-
-        loop(per * len(steps), part)
-
-
-def mix_kernel(start, own_ref, other_ref, *outs):
+            out[block(i, 256)] = picked(row_ref[step : step + 1], x_ref[...], n * size + i * 256, 256)
+
+        loop(size // 256, part)
+
+
+def joined(first, second):
+    n = first.shape[0] // 8
+    both = jnp.concatenate([first.reshape(n, 1, 8, D), second.reshape(n, 1, 8, D)], axis=1)
+    return both.reshape(n * 16, D)
+
+
+def head_kernel(step, row_ref, x_ref, g_ref, out):
+    row = row_ref[step : step + 1]
+
+    def part(i):
+        first = chosen(row, x_ref[...], i * 128, 128)
+        out[block(i, 256)] = joined(first, chosen(row, g_ref[...], i * 128, 128)).astype(BF)
+
+    loop(out.shape[0] // 256, part)
+
+
+def mix_kernel(own_ref, other_ref, *outs):
     n = outs[0].shape[0] // 2
     for i, out in enumerate(outs):
-        out[:n] = own_ref[start + i * n : start + (i + 1) * n]
-        out[n:] = other_ref[start + i * n : start + (i + 1) * n]
+        out[:n] = own_ref[i * n : (i + 1) * n]
+        out[n:] = other_ref[i * n : (i + 1) * n]
 
 
 def turn_kernel(parts, *refs):
@@ -119,7 +135,7 @@
         out[...] = jnp.concatenate([r[c, y] for r in rows for c in range(NC)], axis=0).astype(BF)
 
 
-def home_kernel(step, send, row_ref, col_ref, back_ref, g_hbm, *refs):
+def home_kernel(step, send, double, row_ref, col_ref, back_ref, g_hbm, *refs):
     if send:
         g_out, pack_out, old_ref, new_ref, pack_ref, sems = refs
     else:
@@ -127,18 +143,21 @@
     copies = Copies(sems)
     load = copies.start(g_hbm, old_ref)
     slots, tokens = back_ref.shape[0], old_ref.shape[0]
-    sel = (col_ref[:, step : step + 1] == lax.broadcasted_iota(jnp.int32, (tokens, slots), 1)).astype(BF)
+    spots = col_ref[:, step : step + 1]
+    if double:
+        spots = spots // 8 * 16 + spots % 8
+    sel = (spots == lax.broadcasted_iota(jnp.int32, (tokens, slots), 1)).astype(BF)
     load.wait()
 
     def add(i):
-        cols = block(i, 128)
+        cols = block(i, 512)
         fresh = old_ref[:, cols].astype(F32) + dot(sel, back_ref[:, cols])
         new_ref[:, cols] = fresh.astype(BF)
 
-    loop(D // 128, add)
+    loop(D // 512, add)
     copies.store(new_ref, g_out)
     if send:
-        count = slots // 128
+        count = pack_ref.shape[0] // 128
 
         def chunk(i):
             return pltpu.make_async_copy(
@@ -175,10 +194,10 @@
     loop(count // 4, four)
 
 
-def tiles(ref):
+def tiles(ref, size=8, start=0):
     def load(q):
-        rows = ref[block(q, 32)].astype(F32)
-        return [rows[i * 8 : (i + 1) * 8] for i in range(4)]
+        rows = ref[block(q, 4 * size)].astype(F32)
+        return [rows[i * size + start : i * size + start + 8] for i in range(4)]
 
     return load
 
@@ -193,18 +212,17 @@
             one.wait()
 
         def part(i):
-            take, c = block(i % 4, x_ref.shape[1] // 4), i // 4
-            cols, ups = block(c, 256), pl.ds(pl.multiple_of(H + c * 256, 256), 256)
-            rows = x_ref[e, take]
+            cols, ups = block(i, 256), pl.ds(pl.multiple_of(H + i * 256, 256), 256)
+            rows = x_ref[e]
             gate = dot(rows, w_ref[e, :, cols])
             up = dot(rows, w_ref[e, :, ups])
             s = jax.nn.sigmoid(gate)
             silu = gate * s
-            scratch[1][e, take, cols] = silu.astype(BF)
-            scratch[2][e, take, cols] = (up * s * (1.0 + gate * (1.0 - s))).astype(BF)
-            scratch[3][e, take, cols] = (silu * up).astype(BF)
-
-        loop(4 * (H // 256), part)
+            scratch[1][e, :, cols] = silu.astype(BF)
+            scratch[2][e, :, cols] = (up * s * (1.0 + gate * (1.0 - s))).astype(BF)
+            scratch[3][e, :, cols] = (silu * up).astype(BF)
+
+        loop(H // 256, part)
         for one in copies_of(e, results, sems, experts):
             one.start()
 
@@ -218,6 +236,13 @@
     for e in range(w_ref.shape[0]):
         for one in copies_of(e, [(w_hbm, w_ref)], sems, 0):
             one.start()
+
+
+def x_both_kernel(start, both_ref, w_hbm, *refs):
+    outs, scratch, (w_ref, sems, _) = refs[:4], refs[4:8], refs[8:]
+    load_weights(w_hbm, w_ref, sems)
+    by_expert(tiles(both_ref, 16, start), both_ref.shape[0] // 16, scratch[0])
+    x_math(w_hbm, w_ref, scratch, outs, sems)
 
 
 def x_kernel(parts, where_ref, *refs):
@@ -241,7 +266,9 @@
     x_math(w_hbm, w_ref, scratch, outs, sems)
 
 
-def g_kernel(keep, g_in, silu_hbm, slope_hbm, win_hbm, wout_hbm, *refs):
+def g_kernel(size, more, keep, g_in, silu_hbm, slope_hbm, win_hbm, wout_hbm, *refs):
+    if more:
+        next_ref, refs = refs[0], refs[1:]
     if keep:
         g_ref, pre_ref, back_out = refs[:3]
     else:
@@ -256,32 +283,20 @@
     for e in range(experts):
         for one in copies_of(e, first, sems, 0) + copies_of(e, second, sems, base):
             one.start()
-    by_expert(tiles(g_in), g_in.shape[0] // 8, g_ref)
-
-    def expert(e):
+    by_expert(tiles(g_in, size, size - 8), g_in.shape[0] // size, g_ref)
+    for e in range(experts):
         for one in copies_of(e, first, sems, 0):
             one.wait()
 
-        def inner(i):
-            take, c = block(i % 2, g_ref.shape[1] // 2), i // 2
-            cols, ups = block(c, 256), pl.ds(pl.multiple_of(H + c * 256, 256), 256)
-            grad = dot(g_ref[e, take], wout_ref[e, cols], NT)
-            pre_ref[e, take, cols] = (grad * slope_ref[e, take, cols].astype(F32)).astype(BF)
-            pre_ref[e, take, ups] = (grad * silu_ref[e, take, cols].astype(F32)).astype(BF)
-
-        loop(2 * (H // 256), inner)
+        grad = dot(g_ref[e], wout_ref[e], NT)
+        pre_ref[e, :, :H] = (grad * slope_ref[e].astype(F32)).astype(BF)
+        pre_ref[e, :, H:] = (grad * silu_ref[e].astype(F32)).astype(BF)
         for one in copies_of(e, results, sems, after):
             one.start()
         for one in copies_of(e, second, sems, base):
             one.wait()
 
-        def outer(i):
-            cols = block(i, 256)
-            exp_ref[e, :, cols] = dot(pre_ref[e], win_ref[e, cols], NT)
-
-        loop(D // 256, outer)
-
-    loop(experts, expert)
+        exp_ref[e] = dot(pre_ref[e], win_ref[e], NT)
     low = lax.broadcasted_iota(jnp.int32, (8, D), 0) < 4
     count = exp_ref.shape[1] // 8
     last = after + experts * len(results)
@@ -290,10 +305,14 @@
     def back(q):
         e0, e1 = exp_ref[0, block(q, 8)], exp_ref[1, block(q, 8)]
         a, b = swap_halves(low, e0, e1)
-        back_ref[block(q, 16)] = jnp.concatenate([a, b], axis=0).astype(BF)
+        if more:
+            x = next_ref[block(q, 16)].astype(F32)
+            back_ref[block(q, 32)] = jnp.concatenate([a, x[:8], b, x[8:]], axis=0).astype(BF)
+        else:
+            back_ref[block(q, 16)] = jnp.concatenate([a, b], axis=0).astype(BF)
 
     def piece(i):
-        rows = block(i, 16 * count // pieces)
+        rows = block(i, back_ref.shape[0] // pieces)
         return pltpu.make_async_copy(back_ref.at[rows], back_out.at[rows], sems.at[last + i])
 
     def send(i):
@@ -309,7 +328,7 @@
 
 def grad_kernel(picks, dp, turn_ref, *refs):
     steps = [refs[4 * k : 4 * k + 4] for k in range(STEPS)]
-    adds, outs = refs[4 * STEPS : -2], refs[-2:]
+    outs = refs[-2:]
     rows_in, rows_out = D // dp, H // dp
     (e0, r0), (e1, r1) = picks
 
@@ -318,43 +337,49 @@
         lefts = [(x[e, :, block(place, rows_in)], hid[e, :, block(place, rows_out)]) for x, _, hid, _ in steps]
 
         def part(i):
-            cols = block(i, 256)
+            cols = block(i, 512)
             one = sum(dot(left[0], pre[e, :, cols], TN) for left, (_, pre, _, _) in zip(lefts, steps))
             two = sum(dot(left[1], g[e, :, cols], TN) for left, (_, _, _, g) in zip(lefts, steps))
             for m, out in enumerate(outs):
 
                 @pl.when(n == m)
                 def _():
-                    first, second = one, two
-                    if adds:
-                        first = first + adds[m][:rows_in, cols].astype(F32)
-                        second = second + adds[m][rows_in:, cols].astype(F32)
-                    out[:rows_in, cols] = first.astype(out.dtype)
-                    out[rows_in:, cols] = second.astype(out.dtype)
-
-        loop(D // 256, part)
+                    out[:rows_in, cols] = one.astype(out.dtype)
+                    out[rows_in:, cols] = two.astype(out.dtype)
+
+        loop(D // 512, part)
 
     loop(2, one_slice)
 
 
+def add_kernel(*refs):
+    count = len(refs) // 3
+    for i, out in enumerate(refs[2 * count :]):
+        a, b = refs[2 * i], refs[2 * i + 1]
+
+        def part(j):
+            rows = block(j, 32)
+            out[rows] = (a[rows].astype(F32) + b[rows].astype(F32)).astype(out.dtype)
+
+        loop(out.shape[0] // 32, part)
+
+
 def final_kernel(count, *refs):
-    ins, (win_out, wout_out) = refs[:-2], refs[-2:]
+    ins, (win_out, wout_out, sum_ref, sems) = refs[:-4], refs[-4:]
     rows_in = win_out.shape[1]
+    copies = Copies(sems)
     for e in range(win_out.shape[0]):
         group = ins[e * count : (e + 1) * count]
 
         def part(i):
             rows = block(i, 32)
-            win_out[e, rows] = sum(ref[rows].astype(F32) for ref in group)
+            sum_ref[e, rows] = sum(ref[rows].astype(F32) for ref in group)
 
         loop(rows_in // 32, part)
-
-        def rest(i):
-            rows = block(i, 32)
-            later = pl.ds(pl.multiple_of(rows_in + i * 32, 32), 32)
-            wout_out[e, rows] = sum(ref[later].astype(F32) for ref in group)
-
-        loop(wout_out.shape[1] // 32, rest)
+        copies.store(sum_ref.at[e, :rows_in], win_out.at[e])
+        loop((sum_ref.shape[1] - rows_in) // 32, lambda i: part(rows_in // 32 + i))
+        copies.store(sum_ref.at[e, rows_in:], wout_out.at[e])
+    copies.finish()
 
 
 def program(saved_inputs, cotangent, weight_in, weight_out, expert_ids):
@@ -391,9 +416,9 @@
         out = lax.all_to_all(rows.reshape(peers, per, D), "expert", split_axis=0, concat_axis=0, tiled=True)
         return out.reshape(peers * per, D)
 
-    def pack(steps, where, rows, pieces):
-        outs = (shape((slots * len(steps) // pieces, D), BF),) * pieces
-        return call(functools.partial(pack_kernel, steps), outs, where, rows)
+    def pack(step, where, rows, pieces):
+        outs = (shape((slots // pieces, D), BF),) * pieces
+        return call(functools.partial(pack_kernel, step), outs, where, rows)
 
     def along(pieces, move):
         return [pieces[0]] + [
@@ -409,10 +434,9 @@
     def along_y(pieces):
         return along(pieces, lambda i, d: i // plane * plane + (i // NC + d) % NY * NC + i % NC)
 
-    def mix(pieces, place):
+    def mix(pieces):
         outs = (shape((slots // nz, D), BF),) * nz
-        start = place * slots // NC
-        return call(functools.partial(mix_kernel, start), outs, *pieces)
+        return call(mix_kernel, outs, *pieces)
 
     def turn(pieces):
         outs = (shape((slots // NY, D), BF),) * NY
@@ -430,19 +454,22 @@
         args = (where, *chunks, weight_in)
         return call(kernel, x_shapes, *args, spaces=spaces, out_spaces="hhhh", scratch=x_scratch)
 
-    def g_half(g_in, silu, slope, keep):
-        outs = (
-            shape((exp_dev, per_exp, D), BF),
-            shape((exp_dev, per_exp, 2 * H), BF),
-            shape((slots, D), BF),
-        )
+    def x_both(both, start):
+        kernel = functools.partial(x_both_kernel, start)
+        args = (both, weight_in)
+        return call(kernel, x_shapes, *args, spaces="vh", out_spaces="hhhh", scratch=x_scratch)
+
+    def g_half(g_in, silu, slope, joint=False, following=(), keep=False):
+        back = shape((slots * (1 + len(following)), D), BF)
+        outs = (shape((exp_dev, per_exp, D), BF), shape((exp_dev, per_exp, 2 * H), BF), back)
         own = [] if keep else list(outs[:2])
         scratch = [pltpu.VMEM(s.shape, s.dtype) for s in own + [silu, slope, weight_in, weight_out]]
-        scratch += [pltpu.VMEM((exp_dev, per_exp, D), F32), pltpu.VMEM((slots, D), BF), pltpu.SemaphoreType.DMA((24,))]
-        kernel = functools.partial(g_kernel, keep)
+        scratch += [pltpu.VMEM((exp_dev, per_exp, D), F32), pltpu.VMEM(back.shape, BF), pltpu.SemaphoreType.DMA((24,))]
+        kernel = functools.partial(g_kernel, 16 if joint else 8, len(following) > 0, keep)
         out_spaces = "vvh" if keep else "hhh"
-        args = (g_in, silu, slope, weight_in, weight_out)
-        return call(kernel, outs, *args, spaces="vhhhh", out_spaces=out_spaces, scratch=scratch)
+        args = (g_in, silu, slope, weight_in, weight_out, *following)
+        spaces = "vhhhh" + "v" * len(following)
+        return call(kernel, outs, *args, spaces=spaces, out_spaces=out_spaces, scratch=scratch)
 
     def home(step, send, back, gradient):
         outs = (shape((tokens, D), BF),)
@@ -451,7 +478,7 @@
             outs += (shape((slots, D), BF),)
             scratch.append(pltpu.VMEM((slots, D), BF))
         scratch.append(pltpu.SemaphoreType.DMA((8,)))
-        kernel = functools.partial(home_kernel, step, send)
+        kernel = functools.partial(home_kernel, step, send, back.shape[0] > slots)
         args = (place, column, back, gradient)
         return call(kernel, outs, *args, spaces="vvvh", out_spaces="h" * len(outs), scratch=scratch)
 
@@ -464,41 +491,44 @@
         return lax.optimization_barrier((values, first))[0]
 
     saved = [None] * STEPS
-    (x_pack,) = pack((2,), place, saved_inputs[2], 1)
-    x_in = swap(x_pack)
-    (g_pack,) = pack((2,), place, cotangent, 1)
-    packed = pack((1, 0), place_near, saved_inputs, NC)
+    (both,) = call(functools.partial(head_kernel, 2), (shape((2 * slots, D), BF),), place, saved_inputs[2], cotangent)
+    both = swap(both)
+    x_one = pack(1, place, saved_inputs[1], 1)
+    packed = pack(0, place_near, saved_inputs[0], NC)
     packed = across_cores(packed)
-    pieces = {}
-    for k in (1, 0):
-        pieces[k] = mix(packed, 1 - k)
-    chunks, where = [x_in], sources
-    gradient = cotangent
-    for step in (2, 1, 0):
-        g_in = swap(g_pack)
-        x_rows, silu, slope, hidden = x_half(chunks, where)
-        if step > 0:
-            start = after(pieces[step - 1], hidden)
-            got = along_z(start)
-        if step == 1:
-            column = tick(column)
-        g_rows, pre, out = g_half(g_in, silu, slope, step == 0)
-        saved[step] = (x_rows, pre, hidden, g_rows)
-        if step > 0:
-            returned = swap(out)
-            got = after(got, out)
-            turned_parts = turn(got)
-            chunks, where = along_y(turned_parts), block_of
-            column = tick(column)
-            gradient, g_pack = home(step, True, returned, gradient)
+    pieces = mix(packed)
+    x_rows, silu, slope, hidden = x_both(both, 0)
+    g_rows, pre, out = g_half(both, silu, slope, True, x_one)
+    saved[2] = (x_rows, pre, hidden, g_rows)
+    both = swap(out)
+    gradient, g_pack = home(2, True, both, cotangent)
+
+    g_in = swap(g_pack)
+    x_rows, silu, slope, hidden = x_both(both, 8)
+    pieces = after(pieces, hidden)
+    got = along_z(pieces)
+    column = tick(column)
+    g_rows, pre, out = g_half(g_in, silu, slope)
+    saved[1] = (x_rows, pre, hidden, g_rows)
+    returned = swap(out)
+    got = after(got, out)
+    got = turn(got)
+    chunks = along_y(got)
+    column = tick(column)
+    gradient, g_pack = home(1, True, returned, gradient)
+
+    g_in = swap(g_pack)
+    x_rows, silu, slope, hidden = x_half(chunks, block_of)
+    g_rows, pre, out = g_half(g_in, silu, slope, keep=True)
+    saved[0] = (x_rows, pre, hidden, g_rows)
 
     ahead = [(i, (i + 1) % dp) for i in range(dp)]
     behind = [(i, (i - 1) % dp) for i in range(dp)]
 
-    def parts(picks, adds=(), dtype=BF):
+    def parts(picks, dtype=BF):
         outs = (shape((rows, D), dtype),) * len(picks)
         kernel = functools.partial(grad_kernel, picks, dp)
-        args = [one for step in saved for one in step] + list(adds)
+        args = [one for step in saved for one in step]
         return call(kernel, outs, turns, *args, spaces="s" + "v" * len(args))
 
     def move(rows, way):
@@ -510,15 +540,18 @@
     near = parts(((1, 1), (0, 3)))
     near1 = move(near[0], ahead)
     near0 = move(near[1], behind)
+    last = parts(((0, 1), (1, 3)), F32)
+    own = parts(((0, 0), (1, 0)))
     returned = swap(out)
-    last = parts(((0, 1), (1, 3)), (far0, far1))
+    last = call(add_kernel, (shape((rows, D), BF),) * 2, last[0], far0, last[1], far1)
     last0 = move(last[0], ahead)
     last1 = move(last[1], behind)
-    own = parts(((0, 0), (1, 0)), dtype=F32)
     (gradient,) = home(0, False, returned, gradient)
     outs = (shape((exp_dev, D // dp, D), F32), shape((exp_dev, H // dp, D), F32))
     args = (own[0], near0, last0, own[1], near1, last1)
-    win_grad, wout_grad = call(functools.partial(final_kernel, 3), outs, *args)
+    scratch = [pltpu.VMEM((exp_dev, rows, D), F32), pltpu.SemaphoreType.DMA((4,))]
+    kernel = functools.partial(final_kernel, 3)
+    win_grad, wout_grad = call(kernel, outs, *args, out_spaces="hh", scratch=scratch)
     return (gradient, win_grad, wout_grad)
 
 

time: 432 us -> 385 us (0.89)
  starting transfers between devices: 111 us -> 76.1 us
  Pallas kernels: 86.8 us -> 58.9 us
  waiting for transfers between devices: 213 us -> 228 us
    all_to_all x7 -> x6, waiting for transfers between devices: 101 us -> 150 us  [swap(): lax.all_to_all(rows.reshape(peers, per, D), 'expert', split_axis=0, conca...]
    ppermute x21 -> x11, waiting for transfers between devices: 77.9 us -> 41.8 us  [along(): lax.ppermute(pieces[d], 'expert', [(i, move(i, d)) for i in range(peers)])]
    pallas_call x24 -> x22, Pallas kernels: 86.8 us -> 58.9 us  [call(): pl.pallas_call(kernel, out_shape=outs, in_specs=ins, out_specs=tuple((pl....]
    ppermute x21 -> x11, starting transfers between devices: 45 us -> 21.9 us  [along(): lax.ppermute(pieces[d], 'expert', [(i, move(i, d)) for i in range(peers)])]
    all_to_all x7 -> x6, starting transfers between devices: 56.9 us -> 45.4 us  [swap(): lax.all_to_all(rows.reshape(peers, per, D), 'expert', split_axis=0, conca...]
    unnamed x39 -> x47, local copies, waits for them, and re-layouts: 16.8 us -> 15.6 us
  transfers between devices with their start and end apart: 34 -> 23, of which waited for: 26 -> 17; matrix products, arithmetic and copies ran while one was open for 0% -> 0% of each run, Pallas kernels for 11% -> 7%
where the time goes in v1:
time: 385 us; the launch traced here: 383 us
  waiting for transfers between devices  228 us (59%)
  starting transfers between devices  76.1 us (20%)
  Pallas kernels  58.9 us (15%)
  local copies, waits for them, and re-layouts  18.2 us (5%)
    all_to_all x6, waiting for transfers between devices, swap(): lax.all_to_all(rows.reshape(peers, per, D), 'expert', split_axis=0, conca...  150 us
    pallas_call x22, Pallas kernels, call(): pl.pallas_call(kernel, out_shape=outs, in_specs=ins, out_specs=tuple((pl....  58.9 us
    all_to_all x6, starting transfers between devices, swap(): lax.all_to_all(rows.reshape(peers, per, D), 'expert', split_axis=0, conca...  45.4 us
    ppermute x11, waiting for transfers between devices, along(): lax.ppermute(pieces[d], 'expert', [(i, move(i, d)) for i in range(peers)])  41.8 us
    ppermute x6, waiting for transfers between devices, move(): return lax.ppermute(rows, 'dp', way)  36.6 us
    ppermute x11, starting transfers between devices, along(): lax.ppermute(pieces[d], 'expert', [(i, move(i, d)) for i in range(peers)])  21.9 us
    unnamed x47, local copies, waits for them, and re-layouts  15.6 us
    ppermute x6, starting transfers between devices, move(): return lax.ppermute(rows, 'dp', way)  8.73 us
  transfers between devices with their start and end apart: 23, of which 17 were waited for; matrix products, arithmetic and copies ran while one was open for 0% of the time, Pallas kernels for 7%

profile of v1, /device:TPU:32, one launch (start us, length us, event | category | flops | bytes accessed | tf_op | source)
XLA Modules:
  0.0 383.2 jit_solution(310656575230530368)
XLA Ops:
  6.8 11.8 %all-to-all-start = ((bf16[64,16,1024]{2,1,0:T(8,128)(2,1)}), bf16[64,16,1024]{2,1,0:T(8,128)(2,1)S(1)}, u32[]{:S(2)}, u32[]{:S(2)}) async-start(bf16[64,16,1024]{2,1,0:T(8,128)(2,1)} %bitcast.38), calls=%async_computation | async-start | bytes 4194304 | tf_op jit(solution)/shard_map/all_to_all | solution.py:416
  20.2 48.7 %all-to-all-done = bf16[64,16,1024]{2,1,0:T(8,128)(2,1)S(1)} async-done(((bf16[64,16,1024]{2,1,0:T(8,128)(2,1)}), bf16[64,16,1024]{2,1,0:T(8,128)(2,1)S(1)}, u32[]{:S(2)}, u32[]{:S(2)}) %all-to-all-start) | async-done | bytes 2097184 | tf_op jit(solution)/shard_map/all_to_all | solution.py:416
  69.0 4.7 %shard_map.79 = (bf16[2,256,1024]{2,1,0:T(8,128)(2,1)}, bf16[2,256,512]{2,1,0:T(8,128)(2,1)}, bf16[2,256,512]{2,1,0:T(8,128)(2,1)}, bf16[2,256,512]{2,1,0:T(8,128)(2,1)}) custom-call(bf16[1024,1024]{1,0:T(8,128)(2,1)S(1)} %bitcast.34, bf16[2,1024,1024]{2,1,0:T(8,128)(2,1)} %win_hbm.5), custom_call_target="tpu_custom_call" | custom-call | tf_op jit(solution)/shard_map/pallas_call | solution.py:30
  73.6 5.9 %shard_map.81 = (bf16[2,256,1024]{2,1,0:T(8,128)(2,1)}, bf16[2,256,1024]{2,1,0:T(8,128)(2,1)}, bf16[1024,1024]{1,0:T(8,128)(2,1)}) custom-call(bf16[1024,1024]{1,0:T(8,128)(2,1)S(1)} %bitcast.35, bf16[2,256,512]{2,1,0:T(8,128)(2,1)} %get-tuple-element.70.silu_hbm, bf16[2,256,512]{2,1,0:T(8,128)(2,1)} %get-tuple-element.71.slope_hbm, ...), custom_call_target="tpu_custom_call" | custom-call | tf_op jit(solution)/shard_map/pallas_call | solution.py:30
  79.6 6.3 %all-to-all-start.1 = ((bf16[64,16,1024]{2,1,0:T(8,128)(2,1)}), bf16[64,16,1024]{2,1,0:T(8,128)(2,1)S(1)}, u32[]{:S(2)}, u32[]{:S(2)}) async-start(bf16[64,16,1024]{2,1,0:T(8,128)(2,1)} %bitcast.43), calls=%async_computation.1 | async-start | bytes 4194304 | tf_op jit(solution)/shard_map/all_to_all | solution.py:416
  86.0 50.2 %all-to-all-done.1 = bf16[64,16,1024]{2,1,0:T(8,128)(2,1)S(1)} async-done(((bf16[64,16,1024]{2,1,0:T(8,128)(2,1)}), bf16[64,16,1024]{2,1,0:T(8,128)(2,1)S(1)}, u32[]{:S(2)}, u32[]{:S(2)}) %all-to-all-start.1) | async-done | bytes 2097184 | tf_op jit(solution)/shard_map/all_to_all | solution.py:416
  136.3 3.8 shard_map.82
  140.0 6.3 %all-to-all-start.2 = ((bf16[64,8,1024]{2,1,0:T(8,128)(2,1)}), bf16[64,8,1024]{2,1,0:T(8,128)(2,1)S(1)}, u32[]{:S(2)}, u32[]{:S(2)}) async-start(bf16[64,8,1024]{2,1,0:T(8,128)(2,1)} %bitcast.47), calls=%async_computation.2 | async-start | bytes 2097152 | tf_op jit(solution)/shard_map/all_to_all | solution.py:416
  146.3 4.7 %shard_map.83 = (bf16[2,256,1024]{2,1,0:T(8,128)(2,1)}, bf16[2,256,512]{2,1,0:T(8,128)(2,1)}, bf16[2,256,512]{2,1,0:T(8,128)(2,1)}, bf16[2,256,512]{2,1,0:T(8,128)(2,1)}) custom-call(bf16[1024,1024]{1,0:T(8,128)(2,1)S(1)} %bitcast.37, bf16[2,1024,1024]{2,1,0:T(8,128)(2,1)} %win_hbm.5), custom_call_target="tpu_custom_call" | custom-call | tf_op jit(solution)/shard_map/pallas_call | solution.py:30
  151.0 23.2 %all-to-all-done.2 = bf16[64,8,1024]{2,1,0:T(8,128)(2,1)S(1)} async-done(((bf16[64,8,1024]{2,1,0:T(8,128)(2,1)}), bf16[64,8,1024]{2,1,0:T(8,128)(2,1)S(1)}, u32[]{:S(2)}, u32[]{:S(2)}) %all-to-all-start.2) | async-done | bytes 1048608 | tf_op jit(solution)/shard_map/all_to_all | solution.py:416
  174.2 5.6 %shard_map.84 = (bf16[2,256,1024]{2,1,0:T(8,128)(2,1)}, bf16[2,256,1024]{2,1,0:T(8,128)(2,1)}, bf16[512,1024]{1,0:T(8,128)(2,1)}) custom-call(bf16[512,1024]{1,0:T(8,128)(2,1)S(1)} %bitcast.41, bf16[2,256,512]{2,1,0:T(8,128)(2,1)} %get-tuple-element.74.silu_hbm, bf16[2,256,512]{2,1,0:T(8,128)(2,1)} %get-tuple-element.75.slope_hbm, ...), custom_call_target="tpu_custom_call" | custom-call | tf_op jit(solution)/shard_map/pallas_call | solution.py:30
  179.9 6.5 %all-to-all-start.3 = ((bf16[64,8,1024]{2,1,0:T(8,128)(2,1)}), bf16[64,8,1024]{2,1,0:T(8,128)(2,1)S(1)}, u32[]{:S(2)}, u32[]{:S(2)}) async-start(bf16[64,8,1024]{2,1,0:T(8,128)(2,1)} %bitcast.46), calls=%async_computation.3 | async-start | bytes 2097152 | tf_op jit(solution)/shard_map/all_to_all | solution.py:416
  186.5 27.9 %all-to-all-done.3 = bf16[64,8,1024]{2,1,0:T(8,128)(2,1)S(1)} async-done(((bf16[64,8,1024]{2,1,0:T(8,128)(2,1)}), bf16[64,8,1024]{2,1,0:T(8,128)(2,1)S(1)}, u32[]{:S(2)}, u32[]{:S(2)}) %all-to-all-start.3) | async-done | bytes 1048608 | tf_op jit(solution)/shard_map/all_to_all | solution.py:416
  214.3 3.4 shard_map.85
  217.7 6.6 %all-to-all-start.4 = ((bf16[64,8,1024]{2,1,0:T(8,128)(2,1)}), bf16[64,8,1024]{2,1,0:T(8,128)(2,1)S(1)}, u32[]{:S(2)}, u32[]{:S(2)}) async-start(bf16[64,8,1024]{2,1,0:T(8,128)(2,1)} %bitcast.44), calls=%async_computation.4 | async-start | bytes 2097152 | tf_op jit(solution)/shard_map/all_to_all | solution.py:416
  228.4 3.7 collective-permute-start.2
  232.7 3.0 collective-permute-start.4
  237.6 13.9 %collective-permute-done.1.refs_1_ = bf16[64,1024]{1,0:T(8,128)(2,1)S(1)} collective-permute-done((bf16[64,1024]{1,0:T(8,128)(2,1)S(1)}, bf16[64,1024]{1,0:T(8,128)(2,1)S(1)}, u32[]{:S(2)}, u32[]{:S(2)}) %collective-permute-start.1) | collective-permute-done | bytes 131104 | tf_op jit(solution)/shard_map/ppermute | solution.py:425
  251.4 4.1 %collective-permute-start.6 = (bf16[64,1024]{1,0:T(8,128)(2,1)S(1)}, bf16[64,1024]{1,0:T(8,128)(2,1)S(1)}, u32[]{:S(2)}, u32[]{:S(2)}) collective-permute-start(bf16[64,1024]{1,0:T(8,128)(2,1)S(1)} %get-tuple-element.96), channel_id=1, source_target_pairs={{0,48},{1,49},{2,50},{3,51},{4,52},{5,53},{6,54},{7,55},{8,56},{9,... | collective-permute-start | bytes 393224 | tf_op jit(solution)/shard_map/ppermute | solution.py:425
  255.6 4.6 %collective-permute-done.2.refs_2_ = bf16[64,1024]{1,0:T(8,128)(2,1)S(1)} collective-permute-done((bf16[64,1024]{1,0:T(8,128)(2,1)S(1)}, bf16[64,1024]{1,0:T(8,128)(2,1)S(1)}, u32[]{:S(2)}, u32[]{:S(2)}) %collective-permute-start.2) | collective-permute-done | bytes 131104 | tf_op jit(solution)/shard_map/ppermute | solution.py:425
  261.9 3.5 collective-permute-done.3.refs_3_
  266.4 2.9 collective-permute-done.6.refs_6_
  276.7 8.6 %collective-permute-done.10.refs_3_ = bf16[128,1024]{1,0:T(8,128)(2,1)S(1)} collective-permute-done((bf16[128,1024]{1,0:T(8,128)(2,1)S(1)}, bf16[128,1024]{1,0:T(8,128)(2,1)S(1)}, u32[]{:S(2)}, u32[]{:S(2)}) %collective-permute-start.10) | collective-permute-done | bytes 262176 | tf_op jit(solution)/shard_map/ppermute | solution.py:425
  285.3 3.4 collective-permute-done.8.refs_1_
  288.7 5.2 %shard_map.89 = (bf16[2,256,1024]{2,1,0:T(8,128)(2,1)}, bf16[2,256,512]{2,1,0:T(8,128)(2,1)}, bf16[2,256,512]{2,1,0:T(8,128)(2,1)}, bf16[2,256,512]{2,1,0:T(8,128)(2,1)}) custom-call(s32[64]{0:T(128)S(1)} %fusion.24.where_ref, bf16[128,1024]{1,0:T(8,128)(2,1)S(1)} %get-tuple-element.106.refs_0_, bf16[128,1024]{1,0:T(8,128)(2,1)S(1)} %collective-permute-done.8.refs_1_, ...), custom_call_target="tpu_custom_call" | custom-call | tf_op jit(solution)/shard_map/pallas_call | solution.py:30
  293.9 5.4 %shard_map.90 = (bf16[2,256,1024]{2,1,0:T(8,128)(2,1)S(1)}, bf16[2,256,1024]{2,1,0:T(8,128)(2,1)S(1)}, bf16[512,1024]{1,0:T(8,128)(2,1)}) custom-call(bf16[512,1024]{1,0:T(8,128)(2,1)S(1)} %bitcast.40, bf16[2,256,512]{2,1,0:T(8,128)(2,1)} %get-tuple-element.110.silu_hbm, bf16[2,256,512]{2,1,0:T(8,128)(2,1)} %get-tuple-element.111.slope_hbm, ...), custom_call_target="tpu_custom_call" | custom-call | tf_op jit(solution)/shard_map/pallas_call | solution.py:30
  301.3 8.0 %all-to-all-start.5 = ((bf16[64,8,1024]{2,1,0:T(8,128)(2,1)}), bf16[64,8,1024]{2,1,0:T(8,128)(2,1)}, u32[]{:S(2)}, u32[]{:S(2)}) async-start(bf16[64,8,1024]{2,1,0:T(8,128)(2,1)} %bitcast.45), calls=%async_computation.5 | async-start | bytes 2097152 | tf_op jit(solution)/shard_map/all_to_all | solution.py:416
  329.0 2.9 shard_map.93
  334.0 10.4 %collective-permute-done.12.refs_1_ = bf16[384,1024]{1,0:T(8,128)(2,1)S(1)} collective-permute-done((bf16[384,1024]{1,0:T(8,128)(2,1)S(1)}, bf16[384,1024]{1,0:T(8,128)(2,1)S(1)}, u32[]{:S(2)}, u32[]{:S(2)}) %collective-permute-start.12) | collective-permute-done | bytes 786464 | tf_op jit(solution)/shard_map/ppermute | solution.py:535
  351.4 10.2 %collective-permute-done.11.refs_1_ = bf16[384,1024]{1,0:T(8,128)(2,1)S(1)} collective-permute-done((bf16[384,1024]{1,0:T(8,128)(2,1)S(1)}, bf16[384,1024]{1,0:T(8,128)(2,1)S(1)}, u32[]{:S(2)}, u32[]{:S(2)}) %collective-permute-start.11) | collective-permute-done | bytes 786464 | tf_op jit(solution)/shard_map/ppermute | solution.py:535
  361.6 15.7 %collective-permute-done.14.refs_2_ = bf16[384,1024]{1,0:T(8,128)(2,1)S(1)} collective-permute-done((bf16[384,1024]{1,0:T(8,128)(2,1)S(1)}, bf16[384,1024]{1,0:T(8,128)(2,1)S(1)}, u32[]{:S(2)}, u32[]{:S(2)}) %collective-permute-start.14) | collective-permute-done | bytes 786464 | tf_op jit(solution)/shard_map/ppermute | solution.py:535
  379.2 3.8 shard_map.91
  (89 shorter events, 57.1 us)
Async XLA Ops:
  0.6 3.6 copy-start.21
  6.8 62.1 %all-to-all-start = ((bf16[64,16,1024]{2,1,0:T(8,128)(2,1)}), bf16[64,16,1024]{2,1,0:T(8,128)(2,1)S(1)}, u32[]{:S(2)}, u32[]{:S(2)}) async-start(bf16[64,16,1024]{2,1,0:T(8,128)(2,1)} %bitcast.38), calls=%async_computation | async-start | bytes 4194304 | tf_op jit(solution)/shard_map/all_to_all | solution.py:416
  79.6 56.7 %all-to-all-start.1 = ((bf16[64,16,1024]{2,1,0:T(8,128)(2,1)}), bf16[64,16,1024]{2,1,0:T(8,128)(2,1)S(1)}, u32[]{:S(2)}, u32[]{:S(2)}) async-start(bf16[64,16,1024]{2,1,0:T(8,128)(2,1)} %bitcast.43), calls=%async_computation.1 | async-start | bytes 4194304 | tf_op jit(solution)/shard_map/all_to_all | solution.py:416
  140.0 34.2 %all-to-all-start.2 = ((bf16[64,8,1024]{2,1,0:T(8,128)(2,1)}), bf16[64,8,1024]{2,1,0:T(8,128)(2,1)S(1)}, u32[]{:S(2)}, u32[]{:S(2)}) async-start(bf16[64,8,1024]{2,1,0:T(8,128)(2,1)} %bitcast.47), calls=%async_computation.2 | async-start | bytes 2097152 | tf_op jit(solution)/shard_map/all_to_all | solution.py:416
  179.9 34.5 %all-to-all-start.3 = ((bf16[64,8,1024]{2,1,0:T(8,128)(2,1)}), bf16[64,8,1024]{2,1,0:T(8,128)(2,1)S(1)}, u32[]{:S(2)}, u32[]{:S(2)}) async-start(bf16[64,8,1024]{2,1,0:T(8,128)(2,1)} %bitcast.46), calls=%async_computation.3 | async-start | bytes 2097152 | tf_op jit(solution)/shard_map/all_to_all | solution.py:416
  186.4 37.9 %copy-start.20 = (bf16[256,1024]{1,0:T(8,128)(2,1)S(1)}, bf16[256,1024]{1,0:T(8,128)(2,1)}, u32[]{:S(2)}) copy-start(bf16[256,1024]{1,0:T(8,128)(2,1)} %get-tuple-element.139.x_ref) | copy-start | bytes 1572868
  217.7 76.1 %all-to-all-start.4 = ((bf16[64,8,1024]{2,1,0:T(8,128)(2,1)}), bf16[64,8,1024]{2,1,0:T(8,128)(2,1)S(1)}, u32[]{:S(2)}, u32[]{:S(2)}) async-start(bf16[64,8,1024]{2,1,0:T(8,128)(2,1)} %bitcast.44), calls=%async_computation.4 | async-start | bytes 2097152 | tf_op jit(solution)/shard_map/all_to_all | solution.py:416
  224.7 2.0 collective-permute-start
  226.8 24.6 %collective-permute-start.1 = (bf16[64,1024]{1,0:T(8,128)(2,1)S(1)}, bf16[64,1024]{1,0:T(8,128)(2,1)S(1)}, u32[]{:S(2)}, u32[]{:S(2)}) collective-permute-start(bf16[64,1024]{1,0:T(8,128)(2,1)S(1)} %get-tuple-element.91), channel_id=1, source_target_pairs={{0,8},{1,9},{2,10},{3,11},{4,12},{5,13},{6,14},{7,15},{8,16},{9,17... | collective-permute-start | bytes 393224 | tf_op jit(solution)/shard_map/ppermute | solution.py:425
  228.4 31.8 %collective-permute-start.2 = (bf16[64,1024]{1,0:T(8,128)(2,1)S(1)}, bf16[64,1024]{1,0:T(8,128)(2,1)S(1)}, u32[]{:S(2)}, u32[]{:S(2)}) collective-permute-start(bf16[64,1024]{1,0:T(8,128)(2,1)S(1)} %get-tuple-element.92), channel_id=1, source_target_pairs={{0,16},{1,17},{2,18},{3,19},{4,20},{5,21},{6,22},{7,23},{8,24},{9,... | collective-permute-start | bytes 393224 | tf_op jit(solution)/shard_map/ppermute | solution.py:425
  232.0 33.4 %collective-permute-start.3 = (bf16[64,1024]{1,0:T(8,128)(2,1)S(1)}, bf16[64,1024]{1,0:T(8,128)(2,1)S(1)}, u32[]{:S(2)}, u32[]{:S(2)}) collective-permute-start(bf16[64,1024]{1,0:T(8,128)(2,1)S(1)} %get-tuple-element.93), channel_id=1, source_target_pairs={{0,24},{1,25},{2,26},{3,27},{4,28},{5,29},{6,30},{7,31},{8,32},{9,... | collective-permute-start | bytes 393224 | tf_op jit(solution)/shard_map/ppermute | solution.py:425
  232.7 32.7 %collective-permute-start.4 = (bf16[64,1024]{1,0:T(8,128)(2,1)S(1)}, bf16[64,1024]{1,0:T(8,128)(2,1)S(1)}, u32[]{:S(2)}, u32[]{:S(2)}) collective-permute-start(bf16[64,1024]{1,0:T(8,128)(2,1)S(1)} %get-tuple-element.94), channel_id=1, source_target_pairs={{0,32},{1,33},{2,34},{3,35},{4,36},{5,37},{6,38},{7,39},{8,40},{9,... | collective-permute-start | bytes 393224 | tf_op jit(solution)/shard_map/ppermute | solution.py:425
  235.8 30.6 %collective-permute-start.5 = (bf16[64,1024]{1,0:T(8,128)(2,1)S(1)}, bf16[64,1024]{1,0:T(8,128)(2,1)S(1)}, u32[]{:S(2)}, u32[]{:S(2)}) collective-permute-start(bf16[64,1024]{1,0:T(8,128)(2,1)S(1)} %get-tuple-element.95), channel_id=1, source_target_pairs={{0,40},{1,41},{2,42},{3,43},{4,44},{5,45},{6,46},{7,47},{8,48},{9,... | collective-permute-start | bytes 393224 | tf_op jit(solution)/shard_map/ppermute | solution.py:425
  251.4 17.8 %collective-permute-start.6 = (bf16[64,1024]{1,0:T(8,128)(2,1)S(1)}, bf16[64,1024]{1,0:T(8,128)(2,1)S(1)}, u32[]{:S(2)}, u32[]{:S(2)}) collective-permute-start(bf16[64,1024]{1,0:T(8,128)(2,1)S(1)} %get-tuple-element.96), channel_id=1, source_target_pairs={{0,48},{1,49},{2,50},{3,51},{4,52},{5,53},{6,54},{7,55},{8,56},{9,... | collective-permute-start | bytes 393224 | tf_op jit(solution)/shard_map/ppermute | solution.py:425
  260.1 11.4 %collective-permute-start.7 = (bf16[64,1024]{1,0:T(8,128)(2,1)S(1)}, bf16[64,1024]{1,0:T(8,128)(2,1)S(1)}, u32[]{:S(2)}, u32[]{:S(2)}) collective-permute-start(bf16[64,1024]{1,0:T(8,128)(2,1)S(1)} %get-tuple-element.97), channel_id=1, source_target_pairs={{0,56},{1,57},{2,58},{3,59},{4,60},{5,61},{6,62},{7,63},{8,0},{9,1... | collective-permute-start | bytes 393224 | tf_op jit(solution)/shard_map/ppermute | solution.py:425
  271.6 13.7 %collective-permute-start.10 = (bf16[128,1024]{1,0:T(8,128)(2,1)S(1)}, bf16[128,1024]{1,0:T(8,128)(2,1)S(1)}, u32[]{:S(2)}, u32[]{:S(2)}) collective-permute-start(bf16[128,1024]{1,0:T(8,128)(2,1)S(1)} %get-tuple-element.109), channel_id=1, source_target_pairs={{0,6},{1,7},{2,0},{3,1},{4,2},{5,3},{6,4},{7,5},{8,14},{9,15},{10,... | collective-permute-start | bytes 786440 | tf_op jit(solution)/shard_map/ppermute | solution.py:425
  274.4 14.3 %collective-permute-start.8 = (bf16[128,1024]{1,0:T(8,128)(2,1)S(1)}, bf16[128,1024]{1,0:T(8,128)(2,1)S(1)}, u32[]{:S(2)}, u32[]{:S(2)}) collective-permute-start(bf16[128,1024]{1,0:T(8,128)(2,1)S(1)} %get-tuple-element.107), channel_id=1, source_target_pairs={{0,2},{1,3},{2,4},{3,5},{4,6},{5,7},{6,0},{7,1},{8,10},{9,11},{10,... | collective-permute-start | bytes 786440 | tf_op jit(solution)/shard_map/ppermute | solution.py:425
  274.4 14.3 %collective-permute-start.9 = (bf16[128,1024]{1,0:T(8,128)(2,1)S(1)}, bf16[128,1024]{1,0:T(8,128)(2,1)S(1)}, u32[]{:S(2)}, u32[]{:S(2)}) collective-permute-start(bf16[128,1024]{1,0:T(8,128)(2,1)S(1)} %get-tuple-element.108), channel_id=1, source_target_pairs={{0,4},{1,5},{2,6},{3,7},{4,0},{5,1},{6,2},{7,3},{8,12},{9,13},{10,... | collective-permute-start | bytes 786440 | tf_op jit(solution)/shard_map/ppermute | solution.py:425
  293.9 15.4 %copy-start.2 = (bf16[2,256,1024]{2,1,0:T(8,128)(2,1)S(1)}, bf16[2,256,1024]{2,1,0:T(8,128)(2,1)}, u32[]{:S(2)}) copy-start(bf16[2,256,1024]{2,1,0:T(8,128)(2,1)} %get-tuple-element.122.refs_9_) | copy-start | bytes 3145732
  301.3 8.0 %copy-start = (bf16[2,256,1024]{2,1,0:T(8,128)(2,1)S(1)}, bf16[2,256,1024]{2,1,0:T(8,128)(2,1)}, u32[]{:S(2)}) copy-start(bf16[2,256,1024]{2,1,0:T(8,128)(2,1)} %get-tuple-element.121.refs_8_) | copy-start | bytes 3145732
  301.3 8.0 %copy-start.1 = (bf16[2,256,1024]{2,1,0:T(8,128)(2,1)S(1)}, bf16[2,256,1024]{2,1,0:T(8,128)(2,1)}, u32[]{:S(2)}) copy-start(bf16[2,256,1024]{2,1,0:T(8,128)(2,1)} %get-tuple-element.124.refs_11_) | copy-start | bytes 3145732
  301.3 77.9 %all-to-all-start.5 = ((bf16[64,8,1024]{2,1,0:T(8,128)(2,1)}), bf16[64,8,1024]{2,1,0:T(8,128)(2,1)}, u32[]{:S(2)}, u32[]{:S(2)}) async-start(bf16[64,8,1024]{2,1,0:T(8,128)(2,1)} %bitcast.45), calls=%async_computation.5 | async-start | bytes 2097152 | tf_op jit(solution)/shard_map/all_to_all | solution.py:416
  322.7 21.7 %collective-permute-start.12 = (bf16[384,1024]{1,0:T(8,128)(2,1)S(1)}, bf16[384,1024]{1,0:T(8,128)(2,1)S(1)}, u32[]{:S(2)}, u32[]{:S(2)}) collective-permute-start(bf16[384,1024]{1,0:T(8,128)(2,1)S(1)} %get-tuple-element.128), channel_id=1, source_target_pairs={{0,64},{64,128},{128,192},{192,0},{1,65},{65,129},{129,193},{193,1... | collective-permute-start | bytes 2359304 | tf_op jit(solution)/shard_map/ppermute | solution.py:535
  324.3 20.4 %collective-permute-start.13 = (bf16[384,1024]{1,0:T(8,128)(2,1)S(1)}, bf16[384,1024]{1,0:T(8,128)(2,1)S(1)}, u32[]{:S(2)}, u32[]{:S(2)}) collective-permute-start(bf16[384,1024]{1,0:T(8,128)(2,1)S(1)} %get-tuple-element.130), channel_id=1, source_target_pairs={{0,192},{64,0},{128,64},{192,128},{1,193},{65,1},{129,65},{193,129... | collective-permute-start | bytes 2359304 | tf_op jit(solution)/shard_map/ppermute | solution.py:535
  331.9 29.7 %collective-permute-start.11 = (bf16[384,1024]{1,0:T(8,128)(2,1)S(1)}, bf16[384,1024]{1,0:T(8,128)(2,1)S(1)}, u32[]{:S(2)}, u32[]{:S(2)}) collective-permute-start(bf16[384,1024]{1,0:T(8,128)(2,1)S(1)} %get-tuple-element.126), channel_id=1, source_target_pairs={{0,192},{64,0},{128,64},{192,128},{1,193},{65,1},{129,65},{193,129... | collective-permute-start | bytes 2359304 | tf_op jit(solution)/shard_map/ppermute | solution.py:535
  333.6 28.0 %collective-permute-start.15 = (bf16[384,1024]{1,0:T(8,128)(2,1)S(1)}, bf16[384,1024]{1,0:T(8,128)(2,1)S(1)}, u32[]{:S(2)}, u32[]{:S(2)}) collective-permute-start(bf16[384,1024]{1,0:T(8,128)(2,1)S(1)} %get-tuple-element.133), channel_id=1, source_target_pairs={{0,64},{64,128},{128,192},{192,0},{1,65},{65,129},{129,193},{193,1... | collective-permute-start | bytes 2359304 | tf_op jit(solution)/shard_map/ppermute | solution.py:535
  344.7 3.7 copy-start.4
  344.7 3.7 copy-start.6
  344.7 3.7 copy-start.14
  344.7 3.7 copy-start.16
  345.1 32.2 %collective-permute-start.14 = (bf16[384,1024]{1,0:T(8,128)(2,1)S(1)}, bf16[384,1024]{1,0:T(8,128)(2,1)S(1)}, u32[]{:S(2)}, u32[]{:S(2)}) collective-permute-start(bf16[384,1024]{1,0:T(8,128)(2,1)S(1)} %get-tuple-element.131), channel_id=1, source_target_pairs={{0,64},{64,128},{128,192},{192,0},{1,65},{65,129},{129,193},{193,1... | collective-permute-start | bytes 2359304 | tf_op jit(solution)/shard_map/ppermute | solution.py:535
  346.7 30.6 %collective-permute-start.16 = (bf16[384,1024]{1,0:T(8,128)(2,1)S(1)}, bf16[384,1024]{1,0:T(8,128)(2,1)S(1)}, u32[]{:S(2)}, u32[]{:S(2)}) collective-permute-start(bf16[384,1024]{1,0:T(8,128)(2,1)S(1)} %get-tuple-element.134), channel_id=1, source_target_pairs={{0,192},{64,0},{128,64},{192,128},{1,193},{65,1},{129,65},{193,129... | collective-permute-start | bytes 2359304 | tf_op jit(solution)/shard_map/ppermute | solution.py:535
  (14 other events, 18.4 us)

commit v2 on v1

--- a/solution.py
+++ b/solution.py
@@ -90,7 +90,9 @@
     return chosen(row, rows, start, count).astype(BF)
 
 
-def pack_kernel(step, row_ref, x_ref, *outs):
+def pack_kernel(step, row_ref, x_hbm, *refs):
+    outs, (x_ref, sems) = refs[:-2], refs[-2:]
+    Copies(sems).start(x_hbm.at[step], x_ref).wait()
     for n, out in enumerate(outs):
         size = out.shape[0]
 
@@ -106,14 +108,24 @@
     return both.reshape(n * 16, D)
 
 
-def head_kernel(step, row_ref, x_ref, g_ref, out):
+def head_kernel(step, row_ref, x_hbm, g_hbm, out_hbm, x_ref, g_ref, out_ref, sems):
+    copies = Copies(sems)
+    loads = [copies.start(x_hbm.at[step], x_ref), copies.start(g_hbm, g_ref)]
     row = row_ref[step : step + 1]
+    count = out_ref.shape[0] // 256
+    for load in loads:
+        load.wait()
+
+    def piece(i):
+        return pltpu.make_async_copy(out_ref.at[block(i, 256)], out_hbm.at[block(i, 256)], sems.at[2 + i])
 
     def part(i):
         first = chosen(row, x_ref[...], i * 128, 128)
-        out[block(i, 256)] = joined(first, chosen(row, g_ref[...], i * 128, 128)).astype(BF)
-
-    loop(out.shape[0] // 256, part)
+        out_ref[block(i, 256)] = joined(first, chosen(row, g_ref[...], i * 128, 128)).astype(BF)
+        piece(i).start()
+
+    loop(count, part)
+    loop(count, lambda i: piece(i).wait())
 
 
 def mix_kernel(own_ref, other_ref, *outs):
@@ -416,9 +428,11 @@
         out = lax.all_to_all(rows.reshape(peers, per, D), "expert", split_axis=0, concat_axis=0, tiled=True)
         return out.reshape(peers * per, D)
 
-    def pack(step, where, rows, pieces):
+    def pack(step, where, pieces):
         outs = (shape((slots // pieces, D), BF),) * pieces
-        return call(functools.partial(pack_kernel, step), outs, where, rows)
+        scratch = [pltpu.VMEM((tokens, D), BF), pltpu.SemaphoreType.DMA((1,))]
+        kernel = functools.partial(pack_kernel, step)
+        return call(kernel, outs, where, saved_inputs, spaces="vh", scratch=scratch)
 
     def along(pieces, move):
         return [pieces[0]] + [
@@ -491,10 +505,14 @@
         return lax.optimization_barrier((values, first))[0]
 
     saved = [None] * STEPS
-    (both,) = call(functools.partial(head_kernel, 2), (shape((2 * slots, D), BF),), place, saved_inputs[2], cotangent)
+    outs = (shape((2 * slots, D), BF),)
+    scratch = [pltpu.VMEM((n, D), BF) for n in (tokens, tokens, 2 * slots)] + [pltpu.SemaphoreType.DMA((8,))]
+    args = (place, saved_inputs, cotangent)
+    kernel = functools.partial(head_kernel, 2)
+    (both,) = call(kernel, outs, *args, spaces="vhh", out_spaces="h", scratch=scratch)
     both = swap(both)
-    x_one = pack(1, place, saved_inputs[1], 1)
-    packed = pack(0, place_near, saved_inputs[0], NC)
+    x_one = pack(1, place, 1)
+    packed = pack(0, place_near, NC)
     packed = across_cores(packed)
     pieces = mix(packed)
     x_rows, silu, slope, hidden = x_both(both, 0)

time: 385 us -> 384 us (level)
  local copies, waits for them, and re-layouts: 18.2 us -> 13.4 us
  Pallas kernels: 58.9 us -> 63.1 us
    pallas_call x22, Pallas kernels: 58.9 us -> 63.1 us  [call(): pl.pallas_call(kernel, out_shape=outs, in_specs=ins, out_specs=tuple((pl....]
    unnamed x47 -> x37, local copies, waits for them, and re-layouts: 15.6 us -> 13.2 us
where the time goes in v2:
time: 384 us; the launch traced here: 382 us
  waiting for transfers between devices  227 us (59%)
  starting transfers between devices  76.5 us (20%)
  Pallas kernels  63.1 us (16%)
  local copies, waits for them, and re-layouts  13.4 us (3%)
    all_to_all x6, waiting for transfers between devices, swap(): lax.all_to_all(rows.reshape(peers, per, D), 'expert', split_axis=0, conca...  150 us
    pallas_call x22, Pallas kernels, call(): pl.pallas_call(kernel, out_shape=outs, in_specs=ins, out_specs=tuple((pl....  63.1 us
    all_to_all x6, starting transfers between devices, swap(): lax.all_to_all(rows.reshape(peers, per, D), 'expert', split_axis=0, conca...  45.4 us
    ppermute x11, waiting for transfers between devices, along(): lax.ppermute(pieces[d], 'expert', [(i, move(i, d)) for i in range(peers)])  40.6 us
    ppermute x6, waiting for transfers between devices, move(): return lax.ppermute(rows, 'dp', way)  36.7 us
    ppermute x11, starting transfers between devices, along(): lax.ppermute(pieces[d], 'expert', [(i, move(i, d)) for i in range(peers)])  22.2 us
    unnamed x37, local copies, waits for them, and re-layouts  13.2 us
    ppermute x6, starting transfers between devices, move(): return lax.ppermute(rows, 'dp', way)  8.95 us
  transfers between devices with their start and end apart: 23, of which 17 were waited for; matrix products, arithmetic and copies ran while one was open for 0% of the time, Pallas kernels for 7%

profile of v2, /device:TPU:32, one launch (start us, length us, event | category | flops | bytes accessed | tf_op | source)
XLA Modules:
  0.0 382.4 jit_solution(13714170147298840026)
XLA Ops:
  2.4 3.3 shard_map.78
  5.8 11.8 %all-to-all-start = ((bf16[64,16,1024]{2,1,0:T(8,128)(2,1)}), bf16[64,16,1024]{2,1,0:T(8,128)(2,1)S(1)}, u32[]{:S(2)}, u32[]{:S(2)}) async-start(bf16[64,16,1024]{2,1,0:T(8,128)(2,1)} %bitcast.36), calls=%async_computation | async-start | bytes 4194304 | tf_op jit(solution)/shard_map/all_to_all | solution.py:428
  19.2 48.7 %all-to-all-done = bf16[64,16,1024]{2,1,0:T(8,128)(2,1)S(1)} async-done(((bf16[64,16,1024]{2,1,0:T(8,128)(2,1)}), bf16[64,16,1024]{2,1,0:T(8,128)(2,1)S(1)}, u32[]{:S(2)}, u32[]{:S(2)}) %all-to-all-start) | async-done | bytes 2097184 | tf_op jit(solution)/shard_map/all_to_all | solution.py:428
  67.9 4.7 %shard_map.79 = (bf16[2,256,1024]{2,1,0:T(8,128)(2,1)}, bf16[2,256,512]{2,1,0:T(8,128)(2,1)}, bf16[2,256,512]{2,1,0:T(8,128)(2,1)}, bf16[2,256,512]{2,1,0:T(8,128)(2,1)}) custom-call(bf16[1024,1024]{1,0:T(8,128)(2,1)S(1)} %bitcast.28, bf16[2,1024,1024]{2,1,0:T(8,128)(2,1)} %win_hbm.5), custom_call_target="tpu_custom_call" | custom-call | tf_op jit(solution)/shard_map/pallas_call | solution.py:30
  72.6 5.9 %shard_map.81 = (bf16[2,256,1024]{2,1,0:T(8,128)(2,1)}, bf16[2,256,1024]{2,1,0:T(8,128)(2,1)}, bf16[1024,1024]{1,0:T(8,128)(2,1)}) custom-call(bf16[1024,1024]{1,0:T(8,128)(2,1)S(1)} %bitcast.29, bf16[2,256,512]{2,1,0:T(8,128)(2,1)} %get-tuple-element.70.silu_hbm, bf16[2,256,512]{2,1,0:T(8,128)(2,1)} %get-tuple-element.71.slope_hbm, ...), custom_call_target="tpu_custom_call" | custom-call | tf_op jit(solution)/shard_map/pallas_call | solution.py:30
  78.5 6.3 %all-to-all-start.1 = ((bf16[64,16,1024]{2,1,0:T(8,128)(2,1)}), bf16[64,16,1024]{2,1,0:T(8,128)(2,1)S(1)}, u32[]{:S(2)}, u32[]{:S(2)}) async-start(bf16[64,16,1024]{2,1,0:T(8,128)(2,1)} %bitcast.37), calls=%async_computation.1 | async-start | bytes 4194304 | tf_op jit(solution)/shard_map/all_to_all | solution.py:428
  85.0 50.2 %all-to-all-done.1 = bf16[64,16,1024]{2,1,0:T(8,128)(2,1)S(1)} async-done(((bf16[64,16,1024]{2,1,0:T(8,128)(2,1)}), bf16[64,16,1024]{2,1,0:T(8,128)(2,1)S(1)}, u32[]{:S(2)}, u32[]{:S(2)}) %all-to-all-start.1) | async-done | bytes 2097184 | tf_op jit(solution)/shard_map/all_to_all | solution.py:428
  135.2 3.7 shard_map.82
  139.0 6.3 %all-to-all-start.2 = ((bf16[64,8,1024]{2,1,0:T(8,128)(2,1)}), bf16[64,8,1024]{2,1,0:T(8,128)(2,1)S(1)}, u32[]{:S(2)}, u32[]{:S(2)}) async-start(bf16[64,8,1024]{2,1,0:T(8,128)(2,1)} %bitcast.41), calls=%async_computation.2 | async-start | bytes 2097152 | tf_op jit(solution)/shard_map/all_to_all | solution.py:428
  145.3 4.7 %shard_map.83 = (bf16[2,256,1024]{2,1,0:T(8,128)(2,1)}, bf16[2,256,512]{2,1,0:T(8,128)(2,1)}, bf16[2,256,512]{2,1,0:T(8,128)(2,1)}, bf16[2,256,512]{2,1,0:T(8,128)(2,1)}) custom-call(bf16[1024,1024]{1,0:T(8,128)(2,1)S(1)} %bitcast.31, bf16[2,1024,1024]{2,1,0:T(8,128)(2,1)} %win_hbm.5), custom_call_target="tpu_custom_call" | custom-call | tf_op jit(solution)/shard_map/pallas_call | solution.py:30
  150.0 23.2 %all-to-all-done.2 = bf16[64,8,1024]{2,1,0:T(8,128)(2,1)S(1)} async-done(((bf16[64,8,1024]{2,1,0:T(8,128)(2,1)}), bf16[64,8,1024]{2,1,0:T(8,128)(2,1)S(1)}, u32[]{:S(2)}, u32[]{:S(2)}) %all-to-all-start.2) | async-done | bytes 1048608 | tf_op jit(solution)/shard_map/all_to_all | solution.py:428
  173.2 5.6 %shard_map.84 = (bf16[2,256,1024]{2,1,0:T(8,128)(2,1)}, bf16[2,256,1024]{2,1,0:T(8,128)(2,1)}, bf16[512,1024]{1,0:T(8,128)(2,1)}) custom-call(bf16[512,1024]{1,0:T(8,128)(2,1)S(1)} %bitcast.34, bf16[2,256,512]{2,1,0:T(8,128)(2,1)} %get-tuple-element.74.silu_hbm, bf16[2,256,512]{2,1,0:T(8,128)(2,1)} %get-tuple-element.75.slope_hbm, ...), custom_call_target="tpu_custom_call" | custom-call | tf_op jit(solution)/shard_map/pallas_call | solution.py:30
  178.8 6.5 %all-to-all-start.3 = ((bf16[64,8,1024]{2,1,0:T(8,128)(2,1)}), bf16[64,8,1024]{2,1,0:T(8,128)(2,1)S(1)}, u32[]{:S(2)}, u32[]{:S(2)}) async-start(bf16[64,8,1024]{2,1,0:T(8,128)(2,1)} %bitcast.40), calls=%async_computation.3 | async-start | bytes 2097152 | tf_op jit(solution)/shard_map/all_to_all | solution.py:428
  185.4 27.9 %all-to-all-done.3 = bf16[64,8,1024]{2,1,0:T(8,128)(2,1)S(1)} async-done(((bf16[64,8,1024]{2,1,0:T(8,128)(2,1)}), bf16[64,8,1024]{2,1,0:T(8,128)(2,1)S(1)}, u32[]{:S(2)}, u32[]{:S(2)}) %all-to-all-start.3) | async-done | bytes 1048608 | tf_op jit(solution)/shard_map/all_to_all | solution.py:428
  213.3 3.4 shard_map.85
  216.7 6.5 %all-to-all-start.4 = ((bf16[64,8,1024]{2,1,0:T(8,128)(2,1)}), bf16[64,8,1024]{2,1,0:T(8,128)(2,1)S(1)}, u32[]{:S(2)}, u32[]{:S(2)}) async-start(bf16[64,8,1024]{2,1,0:T(8,128)(2,1)} %bitcast.38), calls=%async_computation.4 | async-start | bytes 2097152 | tf_op jit(solution)/shard_map/all_to_all | solution.py:428
  228.5 3.7 collective-permute-start.2
  232.9 3.0 collective-permute-start.4
  237.6 12.6 %collective-permute-done.1.refs_1_ = bf16[64,1024]{1,0:T(8,128)(2,1)S(1)} collective-permute-done((bf16[64,1024]{1,0:T(8,128)(2,1)S(1)}, bf16[64,1024]{1,0:T(8,128)(2,1)S(1)}, u32[]{:S(2)}, u32[]{:S(2)}) %collective-permute-start.1) | collective-permute-done | bytes 131104 | tf_op jit(solution)/shard_map/ppermute | solution.py:439
  250.2 4.3 %collective-permute-start.6 = (bf16[64,1024]{1,0:T(8,128)(2,1)S(1)}, bf16[64,1024]{1,0:T(8,128)(2,1)S(1)}, u32[]{:S(2)}, u32[]{:S(2)}) collective-permute-start(bf16[64,1024]{1,0:T(8,128)(2,1)S(1)} %get-tuple-element.96), channel_id=1, source_target_pairs={{0,48},{1,49},{2,50},{3,51},{4,52},{5,53},{6,54},{7,55},{8,56},{9,... | collective-permute-start | bytes 393224 | tf_op jit(solution)/shard_map/ppermute | solution.py:439
  254.5 4.6 %collective-permute-done.2.refs_2_ = bf16[64,1024]{1,0:T(8,128)(2,1)S(1)} collective-permute-done((bf16[64,1024]{1,0:T(8,128)(2,1)S(1)}, bf16[64,1024]{1,0:T(8,128)(2,1)S(1)}, u32[]{:S(2)}, u32[]{:S(2)}) %collective-permute-start.2) | collective-permute-done | bytes 131104 | tf_op jit(solution)/shard_map/ppermute | solution.py:439
  260.9 3.2 collective-permute-done.3.refs_3_
  275.6 8.6 %collective-permute-done.10.refs_3_ = bf16[128,1024]{1,0:T(8,128)(2,1)S(1)} collective-permute-done((bf16[128,1024]{1,0:T(8,128)(2,1)S(1)}, bf16[128,1024]{1,0:T(8,128)(2,1)S(1)}, u32[]{:S(2)}, u32[]{:S(2)}) %collective-permute-start.10) | collective-permute-done | bytes 262176 | tf_op jit(solution)/shard_map/ppermute | solution.py:439
  284.2 3.4 collective-permute-done.8.refs_1_
  287.6 5.2 %shard_map.89 = (bf16[2,256,1024]{2,1,0:T(8,128)(2,1)}, bf16[2,256,512]{2,1,0:T(8,128)(2,1)}, bf16[2,256,512]{2,1,0:T(8,128)(2,1)}, bf16[2,256,512]{2,1,0:T(8,128)(2,1)}) custom-call(s32[64]{0:T(128)S(1)} %fusion.24.where_ref, bf16[128,1024]{1,0:T(8,128)(2,1)S(1)} %get-tuple-element.106.refs_0_, bf16[128,1024]{1,0:T(8,128)(2,1)S(1)} %collective-permute-done.8.refs_1_, ...), custom_call_target="tpu_custom_call" | custom-call | tf_op jit(solution)/shard_map/pallas_call | solution.py:30
  292.9 5.4 %shard_map.90 = (bf16[2,256,1024]{2,1,0:T(8,128)(2,1)S(1)}, bf16[2,256,1024]{2,1,0:T(8,128)(2,1)S(1)}, bf16[512,1024]{1,0:T(8,128)(2,1)}) custom-call(bf16[512,1024]{1,0:T(8,128)(2,1)S(1)} %bitcast.33, bf16[2,256,512]{2,1,0:T(8,128)(2,1)} %get-tuple-element.110.silu_hbm, bf16[2,256,512]{2,1,0:T(8,128)(2,1)} %get-tuple-element.111.slope_hbm, ...), custom_call_target="tpu_custom_call" | custom-call | tf_op jit(solution)/shard_map/pallas_call | solution.py:30
  300.4 7.9 %all-to-all-start.5 = ((bf16[64,8,1024]{2,1,0:T(8,128)(2,1)}), bf16[64,8,1024]{2,1,0:T(8,128)(2,1)}, u32[]{:S(2)}, u32[]{:S(2)}) async-start(bf16[64,8,1024]{2,1,0:T(8,128)(2,1)} %bitcast.39), calls=%async_computation.5 | async-start | bytes 2097152 | tf_op jit(solution)/shard_map/all_to_all | solution.py:428
  328.2 2.9 shard_map.93
  333.2 10.5 %collective-permute-done.12.refs_1_ = bf16[384,1024]{1,0:T(8,128)(2,1)S(1)} collective-permute-done((bf16[384,1024]{1,0:T(8,128)(2,1)S(1)}, bf16[384,1024]{1,0:T(8,128)(2,1)S(1)}, u32[]{:S(2)}, u32[]{:S(2)}) %collective-permute-start.12) | collective-permute-done | bytes 786464 | tf_op jit(solution)/shard_map/ppermute | solution.py:553
  350.6 10.2 %collective-permute-done.11.refs_1_ = bf16[384,1024]{1,0:T(8,128)(2,1)S(1)} collective-permute-done((bf16[384,1024]{1,0:T(8,128)(2,1)S(1)}, bf16[384,1024]{1,0:T(8,128)(2,1)S(1)}, u32[]{:S(2)}, u32[]{:S(2)}) %collective-permute-start.11) | collective-permute-done | bytes 786464 | tf_op jit(solution)/shard_map/ppermute | solution.py:553
  360.8 15.7 %collective-permute-done.14.refs_2_ = bf16[384,1024]{1,0:T(8,128)(2,1)S(1)} collective-permute-done((bf16[384,1024]{1,0:T(8,128)(2,1)S(1)}, bf16[384,1024]{1,0:T(8,128)(2,1)S(1)}, u32[]{:S(2)}, u32[]{:S(2)}) %collective-permute-start.14) | collective-permute-done | bytes 786464 | tf_op jit(solution)/shard_map/ppermute | solution.py:553
  378.5 3.8 shard_map.91
  (78 shorter events, 57.4 us)
Async XLA Ops:
  5.8 62.1 %all-to-all-start = ((bf16[64,16,1024]{2,1,0:T(8,128)(2,1)}), bf16[64,16,1024]{2,1,0:T(8,128)(2,1)S(1)}, u32[]{:S(2)}, u32[]{:S(2)}) async-start(bf16[64,16,1024]{2,1,0:T(8,128)(2,1)} %bitcast.36), calls=%async_computation | async-start | bytes 4194304 | tf_op jit(solution)/shard_map/all_to_all | solution.py:428
  78.5 56.7 %all-to-all-start.1 = ((bf16[64,16,1024]{2,1,0:T(8,128)(2,1)}), bf16[64,16,1024]{2,1,0:T(8,128)(2,1)S(1)}, u32[]{:S(2)}, u32[]{:S(2)}) async-start(bf16[64,16,1024]{2,1,0:T(8,128)(2,1)} %bitcast.37), calls=%async_computation.1 | async-start | bytes 4194304 | tf_op jit(solution)/shard_map/all_to_all | solution.py:428
  139.0 34.2 %all-to-all-start.2 = ((bf16[64,8,1024]{2,1,0:T(8,128)(2,1)}), bf16[64,8,1024]{2,1,0:T(8,128)(2,1)S(1)}, u32[]{:S(2)}, u32[]{:S(2)}) async-start(bf16[64,8,1024]{2,1,0:T(8,128)(2,1)} %bitcast.41), calls=%async_computation.2 | async-start | bytes 2097152 | tf_op jit(solution)/shard_map/all_to_all | solution.py:428
  178.8 34.5 %all-to-all-start.3 = ((bf16[64,8,1024]{2,1,0:T(8,128)(2,1)}), bf16[64,8,1024]{2,1,0:T(8,128)(2,1)S(1)}, u32[]{:S(2)}, u32[]{:S(2)}) async-start(bf16[64,8,1024]{2,1,0:T(8,128)(2,1)} %bitcast.40), calls=%async_computation.3 | async-start | bytes 2097152 | tf_op jit(solution)/shard_map/all_to_all | solution.py:428
  216.7 76.2 %all-to-all-start.4 = ((bf16[64,8,1024]{2,1,0:T(8,128)(2,1)}), bf16[64,8,1024]{2,1,0:T(8,128)(2,1)S(1)}, u32[]{:S(2)}, u32[]{:S(2)}) async-start(bf16[64,8,1024]{2,1,0:T(8,128)(2,1)} %bitcast.38), calls=%async_computation.4 | async-start | bytes 2097152 | tf_op jit(solution)/shard_map/all_to_all | solution.py:428
  224.7 2.2 collective-permute-start
  227.0 23.2 %collective-permute-start.1 = (bf16[64,1024]{1,0:T(8,128)(2,1)S(1)}, bf16[64,1024]{1,0:T(8,128)(2,1)S(1)}, u32[]{:S(2)}, u32[]{:S(2)}) collective-permute-start(bf16[64,1024]{1,0:T(8,128)(2,1)S(1)} %get-tuple-element.91), channel_id=1, source_target_pairs={{0,8},{1,9},{2,10},{3,11},{4,12},{5,13},{6,14},{7,15},{8,16},{9,17... | collective-permute-start | bytes 393224 | tf_op jit(solution)/shard_map/ppermute | solution.py:439
  228.5 30.6 %collective-permute-start.2 = (bf16[64,1024]{1,0:T(8,128)(2,1)S(1)}, bf16[64,1024]{1,0:T(8,128)(2,1)S(1)}, u32[]{:S(2)}, u32[]{:S(2)}) collective-permute-start(bf16[64,1024]{1,0:T(8,128)(2,1)S(1)} %get-tuple-element.92), channel_id=1, source_target_pairs={{0,16},{1,17},{2,18},{3,19},{4,20},{5,21},{6,22},{7,23},{8,24},{9,... | collective-permute-start | bytes 393224 | tf_op jit(solution)/shard_map/ppermute | solution.py:439
  232.2 31.8 %collective-permute-start.3 = (bf16[64,1024]{1,0:T(8,128)(2,1)S(1)}, bf16[64,1024]{1,0:T(8,128)(2,1)S(1)}, u32[]{:S(2)}, u32[]{:S(2)}) collective-permute-start(bf16[64,1024]{1,0:T(8,128)(2,1)S(1)} %get-tuple-element.93), channel_id=1, source_target_pairs={{0,24},{1,25},{2,26},{3,27},{4,28},{5,29},{6,30},{7,31},{8,32},{9,... | collective-permute-start | bytes 393224 | tf_op jit(solution)/shard_map/ppermute | solution.py:439
  232.9 31.1 %collective-permute-start.4 = (bf16[64,1024]{1,0:T(8,128)(2,1)S(1)}, bf16[64,1024]{1,0:T(8,128)(2,1)S(1)}, u32[]{:S(2)}, u32[]{:S(2)}) collective-permute-start(bf16[64,1024]{1,0:T(8,128)(2,1)S(1)} %get-tuple-element.94), channel_id=1, source_target_pairs={{0,32},{1,33},{2,34},{3,35},{4,36},{5,37},{6,38},{7,39},{8,40},{9,... | collective-permute-start | bytes 393224 | tf_op jit(solution)/shard_map/ppermute | solution.py:439
  236.0 29.4 %collective-permute-start.5 = (bf16[64,1024]{1,0:T(8,128)(2,1)S(1)}, bf16[64,1024]{1,0:T(8,128)(2,1)S(1)}, u32[]{:S(2)}, u32[]{:S(2)}) collective-permute-start(bf16[64,1024]{1,0:T(8,128)(2,1)S(1)} %get-tuple-element.95), channel_id=1, source_target_pairs={{0,40},{1,41},{2,42},{3,43},{4,44},{5,45},{6,46},{7,47},{8,48},{9,... | collective-permute-start | bytes 393224 | tf_op jit(solution)/shard_map/ppermute | solution.py:439
  250.2 18.0 %collective-permute-start.6 = (bf16[64,1024]{1,0:T(8,128)(2,1)S(1)}, bf16[64,1024]{1,0:T(8,128)(2,1)S(1)}, u32[]{:S(2)}, u32[]{:S(2)}) collective-permute-start(bf16[64,1024]{1,0:T(8,128)(2,1)S(1)} %get-tuple-element.96), channel_id=1, source_target_pairs={{0,48},{1,49},{2,50},{3,51},{4,52},{5,53},{6,54},{7,55},{8,56},{9,... | collective-permute-start | bytes 393224 | tf_op jit(solution)/shard_map/ppermute | solution.py:439
  259.1 11.3 %collective-permute-start.7 = (bf16[64,1024]{1,0:T(8,128)(2,1)S(1)}, bf16[64,1024]{1,0:T(8,128)(2,1)S(1)}, u32[]{:S(2)}, u32[]{:S(2)}) collective-permute-start(bf16[64,1024]{1,0:T(8,128)(2,1)S(1)} %get-tuple-element.97), channel_id=1, source_target_pairs={{0,56},{1,57},{2,58},{3,59},{4,60},{5,61},{6,62},{7,63},{8,0},{9,1... | collective-permute-start | bytes 393224 | tf_op jit(solution)/shard_map/ppermute | solution.py:439
  270.5 13.7 %collective-permute-start.10 = (bf16[128,1024]{1,0:T(8,128)(2,1)S(1)}, bf16[128,1024]{1,0:T(8,128)(2,1)S(1)}, u32[]{:S(2)}, u32[]{:S(2)}) collective-permute-start(bf16[128,1024]{1,0:T(8,128)(2,1)S(1)} %get-tuple-element.109), channel_id=1, source_target_pairs={{0,6},{1,7},{2,0},{3,1},{4,2},{5,3},{6,4},{7,5},{8,14},{9,15},{10,... | collective-permute-start | bytes 786440 | tf_op jit(solution)/shard_map/ppermute | solution.py:439
  273.3 14.3 %collective-permute-start.8 = (bf16[128,1024]{1,0:T(8,128)(2,1)S(1)}, bf16[128,1024]{1,0:T(8,128)(2,1)S(1)}, u32[]{:S(2)}, u32[]{:S(2)}) collective-permute-start(bf16[128,1024]{1,0:T(8,128)(2,1)S(1)} %get-tuple-element.107), channel_id=1, source_target_pairs={{0,2},{1,3},{2,4},{3,5},{4,6},{5,7},{6,0},{7,1},{8,10},{9,11},{10,... | collective-permute-start | bytes 786440 | tf_op jit(solution)/shard_map/ppermute | solution.py:439
  273.3 14.3 %collective-permute-start.9 = (bf16[128,1024]{1,0:T(8,128)(2,1)S(1)}, bf16[128,1024]{1,0:T(8,128)(2,1)S(1)}, u32[]{:S(2)}, u32[]{:S(2)}) collective-permute-start(bf16[128,1024]{1,0:T(8,128)(2,1)S(1)} %get-tuple-element.108), channel_id=1, source_target_pairs={{0,4},{1,5},{2,6},{3,7},{4,0},{5,1},{6,2},{7,3},{8,12},{9,13},{10,... | collective-permute-start | bytes 786440 | tf_op jit(solution)/shard_map/ppermute | solution.py:439
  292.9 15.5 %copy-start.2 = (bf16[2,256,1024]{2,1,0:T(8,128)(2,1)S(1)}, bf16[2,256,1024]{2,1,0:T(8,128)(2,1)}, u32[]{:S(2)}) copy-start(bf16[2,256,1024]{2,1,0:T(8,128)(2,1)} %get-tuple-element.122.refs_9_) | copy-start | bytes 3145732
  300.4 8.0 %copy-start = (bf16[2,256,1024]{2,1,0:T(8,128)(2,1)S(1)}, bf16[2,256,1024]{2,1,0:T(8,128)(2,1)}, u32[]{:S(2)}) copy-start(bf16[2,256,1024]{2,1,0:T(8,128)(2,1)} %get-tuple-element.121.refs_8_) | copy-start | bytes 3145732
  300.4 8.0 %copy-start.1 = (bf16[2,256,1024]{2,1,0:T(8,128)(2,1)S(1)}, bf16[2,256,1024]{2,1,0:T(8,128)(2,1)}, u32[]{:S(2)}) copy-start(bf16[2,256,1024]{2,1,0:T(8,128)(2,1)} %get-tuple-element.124.refs_11_) | copy-start | bytes 3145732
  300.4 78.1 %all-to-all-start.5 = ((bf16[64,8,1024]{2,1,0:T(8,128)(2,1)}), bf16[64,8,1024]{2,1,0:T(8,128)(2,1)}, u32[]{:S(2)}, u32[]{:S(2)}) async-start(bf16[64,8,1024]{2,1,0:T(8,128)(2,1)} %bitcast.39), calls=%async_computation.5 | async-start | bytes 2097152 | tf_op jit(solution)/shard_map/all_to_all | solution.py:428
  308.4 1.2 copy-start.3
  309.6 1.2 copy-start.5
  321.8 21.9 %collective-permute-start.12 = (bf16[384,1024]{1,0:T(8,128)(2,1)S(1)}, bf16[384,1024]{1,0:T(8,128)(2,1)S(1)}, u32[]{:S(2)}, u32[]{:S(2)}) collective-permute-start(bf16[384,1024]{1,0:T(8,128)(2,1)S(1)} %get-tuple-element.128), channel_id=1, source_target_pairs={{0,64},{64,128},{128,192},{192,0},{1,65},{65,129},{129,193},{193,1... | collective-permute-start | bytes 2359304 | tf_op jit(solution)/shard_map/ppermute | solution.py:553
  323.6 20.4 %collective-permute-start.13 = (bf16[384,1024]{1,0:T(8,128)(2,1)S(1)}, bf16[384,1024]{1,0:T(8,128)(2,1)S(1)}, u32[]{:S(2)}, u32[]{:S(2)}) collective-permute-start(bf16[384,1024]{1,0:T(8,128)(2,1)S(1)} %get-tuple-element.130), channel_id=1, source_target_pairs={{0,192},{64,0},{128,64},{192,128},{1,193},{65,1},{129,65},{193,129... | collective-permute-start | bytes 2359304 | tf_op jit(solution)/shard_map/ppermute | solution.py:553
  331.1 29.7 %collective-permute-start.11 = (bf16[384,1024]{1,0:T(8,128)(2,1)S(1)}, bf16[384,1024]{1,0:T(8,128)(2,1)S(1)}, u32[]{:S(2)}, u32[]{:S(2)}) collective-permute-start(bf16[384,1024]{1,0:T(8,128)(2,1)S(1)} %get-tuple-element.126), channel_id=1, source_target_pairs={{0,192},{64,0},{128,64},{192,128},{1,193},{65,1},{129,65},{193,129... | collective-permute-start | bytes 2359304 | tf_op jit(solution)/shard_map/ppermute | solution.py:553
  332.7 28.1 %collective-permute-start.15 = (bf16[384,1024]{1,0:T(8,128)(2,1)S(1)}, bf16[384,1024]{1,0:T(8,128)(2,1)S(1)}, u32[]{:S(2)}, u32[]{:S(2)}) collective-permute-start(bf16[384,1024]{1,0:T(8,128)(2,1)S(1)} %get-tuple-element.133), channel_id=1, source_target_pairs={{0,64},{64,128},{128,192},{192,0},{1,65},{65,129},{129,193},{193,1... | collective-permute-start | bytes 2359304 | tf_op jit(solution)/shard_map/ppermute | solution.py:553
  344.0 3.7 copy-start.4
  344.0 3.7 copy-start.6
  344.0 3.7 copy-start.14
  344.0 3.7 copy-start.16
  344.4 32.1 %collective-permute-start.14 = (bf16[384,1024]{1,0:T(8,128)(2,1)S(1)}, bf16[384,1024]{1,0:T(8,128)(2,1)S(1)}, u32[]{:S(2)}, u32[]{:S(2)}) collective-permute-start(bf16[384,1024]{1,0:T(8,128)(2,1)S(1)} %get-tuple-element.131), channel_id=1, source_target_pairs={{0,64},{64,128},{128,192},{192,0},{1,65},{65,129},{129,193},{193,1... | collective-permute-start | bytes 2359304 | tf_op jit(solution)/shard_map/ppermute | solution.py:553
  345.9 30.6 %collective-permute-start.16 = (bf16[384,1024]{1,0:T(8,128)(2,1)S(1)}, bf16[384,1024]{1,0:T(8,128)(2,1)S(1)}, u32[]{:S(2)}, u32[]{:S(2)}) collective-permute-start(bf16[384,1024]{1,0:T(8,128)(2,1)S(1)} %get-tuple-element.134), channel_id=1, source_target_pairs={{0,192},{64,0},{128,64},{192,128},{1,193},{65,1},{129,65},{193,129... | collective-permute-start | bytes 2359304 | tf_op jit(solution)/shard_map/ppermute | solution.py:553
  (9 other events, 10.1 us)
